TPU v7x, 32 devices: a whole 2x2x4 slice. The times are simulated.
32 devices in a mesh: dp: 16 (over z, y, core), mp: 2 (over x).
Axes of the slice: x: 2, y: 2, z: 4, core: 2. Of those that a mesh axis runs over, the one named last changes fastest.
Arguments:
- tokens: bfloat16 [8000, 1024], P('dp'), may hold values from -6 to 6
- keep_mask: int32 [160, 50], P('dp'), may hold values from 0 to 1, as said below
- ln1_gain: float32 [1024], replicated, may hold values from 0.5 to 1.5
- ln1_bias: float32 [1024], replicated, may hold values from -1.75 to 1.75
- w_qkv: bfloat16 [1024, 3, 1024], P(None, None, 'mp'), may hold values from -0.1875 to 0.1875
- b_qkv: float32 [2, 1024], P(None, 'mp'), may hold values from -3 to 3
- w_proj: bfloat16 [1024, 1024], P('mp'), may hold values from -1 to 1
- b_proj: float32 [1024], replicated, may hold values from -1.75 to 1.75
- ln2_gain: float32 [1024], replicated, may hold values from 0.5 to 1.5
- ln2_bias: float32 [1024], replicated, may hold values from -1.75 to 1.75
- w_fc1: bfloat16 [1024, 4096], P(None, 'mp'), may hold values from -0.1875 to 0.1875
- b_fc1: float32 [4096], P('mp'), may hold values from -3 to 3
- w_fc2: bfloat16 [4096, 1024], P('mp'), may hold values from -0.09375 to 0.09375
- b_fc2: float32 [1024], replicated, may hold values from -1.75 to 1.75
- cotangent: bfloat16 [8000, 1024], P('dp'), may hold values from -6 to 6
Outputs:
- layer_out: bfloat16 [8000, 1024], P('dp')
- grad_tokens: bfloat16 [8000, 1024], P('dp')
- grad_ln1_gain: float32 [1024], replicated
- grad_ln1_bias: float32 [1024], replicated
- grad_w_qkv: float32 [1024, 3, 1024], P(None, None, 'mp')
- grad_b_qkv: float32 [2, 1024], P(None, 'mp')
- grad_w_proj: float32 [1024, 1024], P('mp')
- grad_b_proj: float32 [1024], replicated
- grad_ln2_gain: float32 [1024], replicated
- grad_ln2_bias: float32 [1024], replicated
- grad_w_fc1: float32 [1024, 4096], P(None, 'mp')
- grad_b_fc1: float32 [4096], P('mp')
- grad_w_fc2: float32 [4096, 1024], P('mp')
- grad_b_fc2: float32 [1024], replicated
Inputs may be any that keep to these rules, and one draw needn't show every extreme that they name: `keep_mask`: each image keeps 25 to 50 slots; some image keeps exactly 25 and some all 50.
All inputs are finite; a program needn't handle non-finite values.
Results may differ from a plain program's by a relative error of at most 0.012.
Values sent between devices are 32-bit elements; how exact they have to be, the bound alone decides.
A program may use at most 192 MiB of HBM per device.

v0:
```python
from functools import partial

import jax
import jax.numpy as jnp
from jax import lax
from jax.sharding import PartitionSpec as P

HEAD = 64


def layer_norm(value, gain, shift):
    centered = value - jnp.mean(value, axis=-1, keepdims=True)
    variance = jnp.mean(centered * centered, axis=-1, keepdims=True)
    return centered * lax.rsqrt(variance + 1e-06) * gain + shift


def outer_sum(left, right):
    return lax.dot_general(
        left, right, (((0,), (0,)), ((), ())), preferred_element_type=jnp.float32
    )


def times_transpose(left, right):
    return lax.dot_general(
        left, right, (((1,), (1,)), ((), ())), preferred_element_type=jnp.float32
    )


def body(
    tokens,
    keep_mask,
    ln1_gain,
    ln1_bias,
    w_qkv,
    b_qkv,
    w_proj,
    b_proj,
    ln2_gain,
    ln2_bias,
    w_fc1,
    b_fc1,
    w_fc2,
    b_fc2,
    cotangent,
):
    inputs = tokens.astype(jnp.float32)
    tok_rows, model_width = inputs.shape
    images = keep_mask.shape[0]
    slot_count = tok_rows // images
    local_cols = w_qkv.shape[2]
    local_heads = local_cols // HEAD
    head_shape = (images, slot_count, local_heads, HEAD)
    norm_one_f, norm_one_back = jax.vjp(layer_norm, inputs, ln1_gain, ln1_bias)
    norm_one = norm_one_f.astype(jnp.bfloat16)
    weight_flat = w_qkv.reshape(model_width, 3 * local_cols)
    projected = jnp.dot(norm_one, weight_flat, preferred_element_type=jnp.float32).reshape(
        tok_rows, 3, local_cols
    )
    query = (projected[:, 0] + b_qkv[0]).astype(jnp.bfloat16).reshape(head_shape)
    keys = projected[:, 1].astype(jnp.bfloat16).reshape(head_shape)
    values = (projected[:, 2] + b_qkv[1]).astype(jnp.bfloat16).reshape(head_shape)
    scores = jnp.einsum("bqhd,bkhd->bhqk", query, keys, preferred_element_type=jnp.float32) * 0.125
    live = (keep_mask > 0)[:, None, None, :]
    masked = jnp.where(live, scores, -1e30)
    row_max = jnp.max(masked, axis=-1, keepdims=True)
    exp_terms = jnp.where(live, jnp.exp(masked - row_max), 0.0)
    probs = exp_terms / jnp.sum(exp_terms, axis=-1, keepdims=True)
    probs_low = probs.astype(jnp.bfloat16)
    mixed = jnp.einsum("bhqk,bkhd->bqhd", probs_low, values, preferred_element_type=jnp.float32)
    heads_out = mixed.reshape(tok_rows, local_cols).astype(jnp.bfloat16)
    attn_part = jnp.dot(heads_out, w_proj, preferred_element_type=jnp.float32)
    after_attn = inputs + lax.psum(attn_part, "mp") + b_proj
    norm_two_f, norm_two_back = jax.vjp(layer_norm, after_attn, ln2_gain, ln2_bias)
    norm_two = norm_two_f.astype(jnp.bfloat16)
    pre_act = jnp.dot(norm_two, w_fc1, preferred_element_type=jnp.float32) + b_fc1
    hidden_f, gelu_back = jax.vjp(partial(jax.nn.gelu, approximate=False), pre_act)
    hidden = hidden_f.astype(jnp.bfloat16)
    mlp_part = jnp.dot(hidden, w_fc2, preferred_element_type=jnp.float32)
    final = after_attn + lax.psum(mlp_part, "mp") + b_fc2
    layer_out = final.astype(jnp.bfloat16)
    grad_out = cotangent.astype(jnp.float32)
    grad_b_fc2 = jnp.sum(grad_out, axis=0)
    grad_w_fc2 = outer_sum(hidden, cotangent)
    grad_hidden = times_transpose(cotangent, w_fc2)
    grad_pre = gelu_back(grad_hidden)[0].astype(jnp.bfloat16)
    grad_w_fc1 = outer_sum(norm_two, grad_pre)
    grad_b_fc1 = jnp.sum(grad_pre.astype(jnp.float32), axis=0)
    norm_two_part = times_transpose(grad_pre, w_fc1)
    grad_norm_two = lax.psum(norm_two_part, "mp")
    grad_through, grad_ln2_gain, grad_ln2_bias = norm_two_back(grad_norm_two)
    grad_mid = grad_out + grad_through
    grad_b_proj = jnp.sum(grad_mid, axis=0)
    grad_mid_low = grad_mid.astype(jnp.bfloat16)
    grad_w_proj = outer_sum(heads_out, grad_mid_low)
    grad_heads = times_transpose(grad_mid_low, w_proj).astype(jnp.bfloat16).reshape(head_shape)
    grad_probs = jnp.einsum(
        "bqhd,bkhd->bhqk", grad_heads, values, preferred_element_type=jnp.float32
    )
    grad_values = jnp.einsum(
        "bhqk,bqhd->bkhd", probs_low, grad_heads, preferred_element_type=jnp.float32
    ).astype(jnp.bfloat16)
    inner = jnp.sum(probs * grad_probs, axis=-1, keepdims=True)
    grad_scores = (probs * (grad_probs - inner)).astype(jnp.bfloat16)
    grad_query = (
        jnp.einsum("bhqk,bkhd->bqhd", grad_scores, keys, preferred_element_type=jnp.float32) * 0.125
    ).astype(jnp.bfloat16)
    grad_keys = (
        jnp.einsum("bhqk,bqhd->bkhd", grad_scores, query, preferred_element_type=jnp.float32)
        * 0.125
    ).astype(jnp.bfloat16)
    grad_query = grad_query.reshape(tok_rows, local_cols)
    grad_keys = grad_keys.reshape(tok_rows, local_cols)
    grad_values = grad_values.reshape(tok_rows, local_cols)
    grad_projected = jnp.stack([grad_query, grad_keys, grad_values], axis=1).reshape(
        tok_rows, 3 * local_cols
    )
    grad_w_qkv = outer_sum(norm_one, grad_projected).reshape(model_width, 3, local_cols)
    grad_b_qkv = jnp.stack(
        [
            jnp.sum(grad_query.astype(jnp.float32), axis=0),
            jnp.sum(grad_values.astype(jnp.float32), axis=0),
        ]
    )
    norm_one_part = times_transpose(grad_projected, weight_flat)
    grad_norm_one = lax.psum(norm_one_part, "mp")
    grad_input, grad_ln1_gain, grad_ln1_bias = norm_one_back(grad_norm_one)
    grad_tokens = (grad_mid + grad_input).astype(jnp.bfloat16)
    (
        grad_ln1_gain,
        grad_ln1_bias,
        grad_w_qkv,
        grad_b_qkv,
        grad_w_proj,
        grad_b_proj,
        grad_ln2_gain,
        grad_ln2_bias,
        grad_w_fc1,
        grad_b_fc1,
        grad_w_fc2,
        grad_b_fc2,
    ) = lax.psum(
        (
            grad_ln1_gain,
            grad_ln1_bias,
            grad_w_qkv,
            grad_b_qkv,
            grad_w_proj,
            grad_b_proj,
            grad_ln2_gain,
            grad_ln2_bias,
            grad_w_fc1,
            grad_b_fc1,
            grad_w_fc2,
            grad_b_fc2,
        ),
        "dp",
    )
    return (
        layer_out,
        grad_tokens,
        grad_ln1_gain,
        grad_ln1_bias,
        grad_w_qkv,
        grad_b_qkv,
        grad_w_proj,
        grad_b_proj,
        grad_ln2_gain,
        grad_ln2_bias,
        grad_w_fc1,
        grad_b_fc1,
        grad_w_fc2,
        grad_b_fc2,
    )


def solution(mesh):
    return jax.shard_map(
        body,
        mesh=mesh,
        in_specs=(
            P("dp", None),
            P("dp", None),
            P(),
            P(),
            P(None, None, "mp"),
            P(None, "mp"),
            P("mp", None),
            P(),
            P(),
            P(),
            P(None, "mp"),
            P("mp"),
            P("mp", None),
            P(),
            P("dp", None),
        ),
        out_specs=(
            P("dp", None),
            P("dp", None),
            P(),
            P(),
            P(None, None, "mp"),
            P(None, "mp"),
            P("mp", None),
            P(),
            P(),
            P(),
            P(None, "mp"),
            P("mp"),
            P("mp", None),
            P(),
        ),
        check_vma=False,
    )
```

profile of v0, /device:TPU:0, one launch (start us, length us, event | category | flops | bytes accessed | tf_op | source)
XLA Modules:
  0.0 805.5 jit_solution(2758614402945351057)
XLA Ops:
  10.4 4.7 copy.37
  15.2 3.9 fusion.7
  23.9 2.7 squeeze.7
  29.8 4.4 fusion.63
  39.8 64.8 %all-reduce.8.cloned.1.call-done = f32[500,1024]{1,0:T(8,128)} async-done(((f32[500,1024]{1,0:T(8,128)}), f32[500,1024]{1,0:T(8,128)}) %all-reduce.8.cloned.1.call-update) | async-done | bytes 2048016 | tf_op jit(solution)/shard_map/psum | solution.py:72
  107.8 2.6 fusion.55
  110.5 13.1 %convert_reduce_fusion = (f32[2048]{0:T(1024)S(1)}, bf16[500,2048]{1,0:T(8,128)(2,1)S(1)}, f32[500,2048]{1,0:T(8,128)}) fusion(f32[500,2048]{1,0:T(8,128)S(1)} %fusion.55, f32[2048]{0:T(1024)S(1)} %copy-done.34, bf16[500,1024]{1,0:T(8,128)(2,1)S(1)} %copy-done.16, bf16[2048,1024]{1,0:T(8,128)(2,1)S(1)} %copy-done.39), kind=kOutput, calls=%fused_computation.3 | convolution fusion | flops 2173949952 | bytes 15474688 | tf_op jit(solution)/shard_map/dot_general | solution.py:24
  124.9 3.6 fusion.74
  128.7 4.6 multiply_convert_fusion
  134.5 3.6 fusion.73
  138.2 52.8 %all-reduce.10.cloned.1.call-done = f32[500,1024]{1,0:T(8,128)} async-done(((f32[500,1024]{1,0:T(8,128)}), f32[500,1024]{1,0:T(8,128)}) %all-reduce.10.cloned.1.call-update) | async-done | bytes 2048016 | tf_op jit(solution)/shard_map/psum | solution.py:89
  197.2 2.5 reshape.138
  199.8 3.9 convert_reduce_fusion.3
  219.4 5.0 convolution_bitcast_fusion
  225.7 7.5 fusion.75
  233.2 6.1 fusion.54
  241.6 4.8 fusion.22
  246.6 84.8 %all-reduce.14.cloned.1.call-done = (f32[500,1024]{1,0:T(8,128)}, f32[500,1024]{1,0:T(8,128)}) async-done(((f32[500,1024]{1,0:T(8,128)}, f32[500,1024]{1,0:T(8,128)}), (f32[500,1024]{1,0:T(8,128)}, f32[500,1024]{1,0:T(8,128)})) %all-reduce.14.cloned.1.call-update) | async-done | bytes 4096016 | tf_op jit(solution)/shard_map/psum | solution.py:79
  337.6 65.4 %all-reduce = (f32[1024]{0:T(1024)}, f32[1024]{0:T(1024)}, f32[2,512]{1,0:T(2,128)}, f32[1024]{0:T(1024)}, f32[1024]{0:T(1024)}, /*index=5*/f32[1024]{0:T(1024)}, f32[2048]{0:T(1024)}, f32[1024]{0:T(1024)}) all-reduce(f32[1024]{0:T(1024)S(1)} %get-tuple-element.16, ...), channel_id=1, replica_groups=mesh['dp'=16,'mp'=2] {'dp'}, use_global_device_ids=true, to_apply=%region_16.17 | all-reduce | flops 9216 | bytes 73728 | tf_op jit(solution)/shard_map/psum | solution.py:141
  403.0 3.1 add_convert_fusion.2
  406.1 374.7 %all-reduce.12.cloned.1.call-done = (f32[1024,3,512]{2,0,1:T(8,128)}, f32[512,1024]{1,0:T(8,128)}, f32[1024,2048]{1,0:T(8,128)}, f32[2048,1024]{1,0:T(8,128)}) async-done(((f32[1024,3,512]{2,0,1:T(8,128)}, f32[512,1024]{1,0:T(8,128)}, f32[1024,2048]{1,0:T(8,128)}, f32[2048,1024]{1,0:T(8,128)}), (f32[1024,3,512]{2,0,1:T(8,128)}, f32[512,1024]{1,0:T(8,128)}, f32[1024,2048]{1,0:T(8,128)}, ...) | async-done | bytes 25165840 | tf_op jit(solution)/shard_map/psum | solution.py:141
  780.7 6.9 copy.101
  789.3 4.3 copy.103
  795.1 3.4 copy.104
  (153 shorter events, 57.6 us)
Async XLA Ops:
  7.2 30.3 %copy-start = (bf16[512,1024]{1,0:T(8,128)(2,1)S(1)}, bf16[512,1024]{1,0:T(8,128)(2,1)}, u32[]{:S(2)}) copy-start(bf16[512,1024]{1,0:T(8,128)(2,1)} %param.21) | copy-start | bytes 3145732
  7.2 97.4 %all-reduce.8.cloned.1.call-start = ((), (), s32[]{:S(2)}) async-start(), calls=%async_computation | async-start | bytes 4128768 | tf_op jit(solution)/shard_map/psum | solution.py:72
  10.4 4.8 copy-start.2
  10.4 4.7 copy-start.31
  10.4 4.7 copy-start.42
  29.8 4.5 copy-start.25
  37.5 67.1 %copy-start.36 = (f32[1024]{0:T(1024)S(1)}, f32[1024]{0:T(1024)}, u32[]{:S(2)}) copy-start(f32[1024]{0:T(1024)} %param.22) | copy-start | bytes 12292
  39.6 151.4 %all-reduce.10.cloned.1.call-start = ((), (), s32[]{:S(2)}) async-start(), calls=%async_computation.1 | async-start | bytes 4128768 | tf_op jit(solution)/shard_map/psum | solution.py:89
  110.4 13.1 %copy-start.15 = (f32[500,2048]{1,0:T(8,128)}, f32[500,2048]{1,0:T(8,128)S(1)}, u32[]{:S(2)}) copy-start(f32[500,2048]{1,0:T(8,128)S(1)} %fusion.55) | copy-start | bytes 12288004
  128.6 202.8 %all-reduce.14.cloned.1.call-start = ((), (), s32[]{:S(2)}) async-start(), calls=%async_computation.3 | async-start | bytes 8257536 | tf_op jit(solution)/shard_map/psum | solution.py:79
  128.6 5.9 copy-start.40
  199.8 3.9 copy-start.21
  199.8 3.9 copy-start.26
  199.8 3.9 copy-start.28
  224.5 556.3 %all-reduce.12.cloned.1.call-start = ((), (), s32[]{:S(2)}) async-start(), calls=%async_computation.2 | async-start | bytes 50331648 | tf_op jit(solution)/shard_map/psum | solution.py:141
  225.7 7.5 copy-start.44
  233.2 6.1 copy-start.6
  233.2 6.1 copy-start.12
  233.2 6.1 copy-start.19
  335.6 67.4 %copy-start.37 = (f32[1024]{0:T(1024)S(1)}, f32[1024]{0:T(1024)}, u32[]{:S(2)}) copy-start(f32[1024]{0:T(1024)} %param.28) | copy-start | bytes 12292
  780.7 6.9 copy-start.22
  780.7 8.6 %copy-start.8 = (f32[1024,2048]{1,0:T(8,128)S(1)}, f32[1024,2048]{1,0:T(8,128)}, u32[]{:S(2)}) copy-start(f32[1024,2048]{1,0:T(8,128)} %get-tuple-element.67) | copy-start | bytes 25165828
  787.6 5.9 slice-start
  789.3 5.8 slice-start.1
  (27 other events, 50.2 us)
Sparse Core Ops, SparseCore 0:
  39.7 64.8 all-reduce.7
  128.7 62.1 all-reduce.9
  224.6 106.8 all-reduce.13
  337.3 443.3 all-reduce.11
where the time goes:
time: 812 us; the launch traced here: 805 us
  waiting for transfers between devices  577 us (71%)
  matrix products  70.5 us (9%)
  blocking collectives  65.4 us (8%)
  local copies, waits for them, and re-layouts  53.3 us (7%)
  other arithmetic  24 us (3%)
  between operations  14.6 us (2%)
    psum x1, waiting for transfers between devices, body(): lax.psum((grad_ln1_gain, grad_ln1_bias, grad_w_qkv, grad_b_qkv, grad_w_pr...  375 us
    psum x1, waiting for transfers between devices, body(): final = after_attn + lax.psum(mlp_part, 'mp') + b_fc2  84.8 us
    psum x1, blocking collectives, body(): lax.psum((grad_ln1_gain, grad_ln1_bias, grad_w_qkv, grad_b_qkv, grad_w_pr...  65.4 us
    psum x1, waiting for transfers between devices, body(): after_attn = inputs + lax.psum(attn_part, 'mp') + b_proj  64.8 us
    psum x1, waiting for transfers between devices, body(): grad_norm_two = lax.psum(norm_two_part, 'mp')  52.8 us
    unnamed x101, local copies, waits for them, and re-layouts  35.1 us
    dot_general x4, matrix products, times_transpose(): lax.dot_general(left, right, (((1,), (1,)), ((), ())), preferred_element_...  23.4 us
    dot_general x4, matrix products, outer_sum(): lax.dot_general(left, right, (((0,), (0,)), ((), ())), preferred_element_...  20.7 us
  transfers between devices with their start and end apart: 4, of which 4 were waited for; matrix products, arithmetic and copies ran while one was open for 5% of the time, Pallas kernels for 0%

commit v1 on v0

v1 whole, which is shorter than its diff:
```python
import jax
import jax.numpy as jnp
from jax import lax
from jax.sharding import PartitionSpec as P

HEAD = 64
BF16 = jnp.bfloat16
F32 = jnp.float32


def dot_nn(left, right):
    return jnp.dot(left, right, preferred_element_type=F32)


def dot_tn(left, right):
    return lax.dot_general(left, right, (((0,), (0,)), ((), ())), preferred_element_type=F32)


def dot_nt(left, right):
    return lax.dot_general(left, right, (((1,), (1,)), ((), ())), preferred_element_type=F32)


def norm_parts(value):
    centered = value - jnp.mean(value, axis=-1, keepdims=True)
    variance = jnp.mean(centered * centered, axis=-1, keepdims=True)
    inverse = lax.rsqrt(variance + 1e-06)
    return centered * inverse, inverse


def norm_back(grad, normalized, inverse, gain):
    scaled = grad * gain
    mean_one = jnp.mean(scaled, axis=-1, keepdims=True)
    mean_two = jnp.mean(scaled * normalized, axis=-1, keepdims=True)
    return inverse * (scaled - mean_one - normalized * mean_two)


def swap(value, axis, size, mask):
    return lax.ppermute(value, axis, [(i, i ^ mask) for i in range(size)])


def take_half(value, bit):
    half = value.shape[0] // 2
    return lax.dynamic_slice_in_dim(value, bit * half, half, 0)


def halve(value, bits, masks, size):
    for mask in masks:
        bit = bits[mask]
        sent = swap(take_half(value, 1 - bit), "dp", size, mask)
        value = take_half(value, bit) + sent
    return value


def double(value, bits, masks, size):
    for mask in reversed(masks):
        other = swap(value, "dp", size, mask)
        first = bits[mask] == 0
        value = jnp.where(
            jnp.stack([first, ~first])[:, None, None], value[None], other[None]
        ).reshape(2 * value.shape[0], value.shape[1])
    return value


def make_body(n_dp, n_mp):
    masks = [1 << k for k in range(n_dp.bit_length() - 1)]

    def sum_mp(part):
        if n_mp == 2:
            return part + swap(part, "mp", 2, 1)
        return lax.psum(part, "mp")

    def body(
        tokens, keep_mask, ln1_gain, ln1_bias, w_qkv, b_qkv, w_proj, b_proj,
        ln2_gain, ln2_bias, w_fc1, b_fc1, w_fc2, b_fc2, cotangent,
    ):
        dp_at = lax.axis_index("dp")
        bits = {mask: (dp_at // mask) % 2 for mask in masks}
        order_y = masks
        order_z = masks[:1] + masks[2:] + masks[1:2]

        def sum_outer(left, right, split):
            total = []
            for start, stop, order in ((0, split, order_y), (split, left.shape[1], order_z)):
                if stop == start:
                    continue
                piece = left[:, start:stop]
                half = (stop - start) // 2
                bit = bits[order[0]]
                away = lax.dynamic_slice_in_dim(piece, (1 - bit) * half, half, 1)
                here = lax.dynamic_slice_in_dim(piece, bit * half, half, 1)
                got = swap(dot_tn(away, right), "dp", n_dp, order[0])
                value = dot_tn(here, right) + got
                value = halve(value, bits, order[1:], n_dp)
                total.append(double(value, bits, order, n_dp))
            return jnp.concatenate(total, axis=0) if len(total) > 1 else total[0]

        def sum_small(value):
            for mask in masks:
                value = value + swap(value, "dp", n_dp, mask)
            return value

        inputs = tokens.astype(F32)
        tok_rows, width = inputs.shape
        images = keep_mask.shape[0]
        slots = tok_rows // images
        cols = w_qkv.shape[2]
        heads = cols // HEAD
        shape = (images, slots, heads, HEAD)

        normal_one, inverse_one = norm_parts(inputs)
        norm_one = (normal_one * ln1_gain + ln1_bias).astype(BF16)
        weight = w_qkv.transpose(1, 0, 2)
        query = (dot_nn(norm_one, weight[0]) + b_qkv[0]).astype(BF16).reshape(shape)
        keys = dot_nn(norm_one, weight[1]).astype(BF16).reshape(shape)
        values = (dot_nn(norm_one, weight[2]) + b_qkv[1]).astype(BF16).reshape(shape)
        scores = jnp.einsum("bqhd,bkhd->bhqk", query, keys, preferred_element_type=F32) * 0.125
        live = (keep_mask > 0)[:, None, None, :]
        masked = jnp.where(live, scores, -1e30)
        row_max = jnp.max(masked, axis=-1, keepdims=True)
        exp_terms = jnp.where(live, jnp.exp(masked - row_max), 0.0)
        probs = exp_terms / jnp.sum(exp_terms, axis=-1, keepdims=True)
        probs_low = probs.astype(BF16)
        mixed = jnp.einsum("bhqk,bkhd->bqhd", probs_low, values, preferred_element_type=F32)
        heads_out = mixed.reshape(tok_rows, cols).astype(BF16)
        after_attn = inputs + sum_mp(dot_nn(heads_out, w_proj)) + b_proj

        normal_two, inverse_two = norm_parts(after_attn)
        norm_two = (normal_two * ln2_gain + ln2_bias).astype(BF16)
        pre_act = dot_nn(norm_two, w_fc1) + b_fc1
        hidden_f, gelu_back = jax.vjp(lambda v: jax.nn.gelu(v, approximate=False), pre_act)
        hidden = hidden_f.astype(BF16)
        grad_w_fc2 = sum_outer(hidden, cotangent, hidden.shape[1] * 5 // 8)
        grad_pre = gelu_back(dot_nt(cotangent, w_fc2))[0].astype(BF16)
        grad_norm_two = sum_mp(dot_nt(grad_pre, w_fc1))
        grad_w_fc1 = sum_outer(norm_two, grad_pre, width * 5 // 8)
        mlp_sum = sum_mp(dot_nn(hidden, w_fc2))
        layer_out = (after_attn + mlp_sum + b_fc2).astype(BF16)

        grad_out = cotangent.astype(F32)
        grad_mid = grad_out + norm_back(grad_norm_two, normal_two, inverse_two, ln2_gain)
        grad_mid_low = grad_mid.astype(BF16)
        grad_heads = dot_nt(grad_mid_low, w_proj).astype(BF16).reshape(shape)
        grad_w_proj = sum_outer(heads_out, grad_mid_low, cols)
        grad_probs = jnp.einsum("bqhd,bkhd->bhqk", grad_heads, values, preferred_element_type=F32)
        grad_values = jnp.einsum(
            "bhqk,bqhd->bkhd", probs_low, grad_heads, preferred_element_type=F32
        ).astype(BF16)
        inner = jnp.sum(probs * grad_probs, axis=-1, keepdims=True)
        grad_scores = (probs * (grad_probs - inner)).astype(BF16)
        grad_query = (
            jnp.einsum("bhqk,bkhd->bqhd", grad_scores, keys, preferred_element_type=F32) * 0.125
        ).astype(BF16)
        grad_keys = (
            jnp.einsum("bhqk,bqhd->bkhd", grad_scores, query, preferred_element_type=F32) * 0.125
        ).astype(BF16)
        grad_query = grad_query.reshape(tok_rows, cols)
        grad_keys = grad_keys.reshape(tok_rows, cols)
        grad_values = grad_values.reshape(tok_rows, cols)
        part = (
            dot_nt(grad_query, weight[0])
            + dot_nt(grad_keys, weight[1])
            + dot_nt(grad_values, weight[2])
        )
        grad_norm_one = sum_mp(part)
        grad_w_qkv = jnp.stack(
            [
                sum_outer(norm_one, grad_query, width),
                sum_outer(norm_one, grad_keys, 0),
                sum_outer(norm_one, grad_values, width * 3 // 4),
            ],
            axis=1,
        )
        grad_tokens = (
            grad_mid + norm_back(grad_norm_one, normal_one, inverse_one, ln1_gain)
        ).astype(BF16)

        early = sum_small(
            jnp.concatenate(
                [
                    jnp.sum(grad_out, axis=0),
                    jnp.sum(grad_norm_two * normal_two, axis=0),
                    jnp.sum(grad_norm_two, axis=0),
                    jnp.sum(grad_mid, axis=0),
                    jnp.sum(grad_pre.astype(F32), axis=0),
                    jnp.sum(grad_query.astype(F32), axis=0),
                    jnp.sum(grad_values.astype(F32), axis=0),
                ]
            ).reshape(-1, 128)
        ).reshape(-1)
        late = sum_small(
            jnp.concatenate(
                [jnp.sum(grad_norm_one * normal_one, axis=0), jnp.sum(grad_norm_one, axis=0)]
            ).reshape(-1, 128)
        ).reshape(-1)
        spot = 4 * width + b_fc1.shape[0]
        return (
            layer_out,
            grad_tokens,
            late[:width],
            late[width:],
            grad_w_qkv,
            early[spot:].reshape(2, cols),
            grad_w_proj,
            early[3 * width : 4 * width],
            early[width : 2 * width],
            early[2 * width : 3 * width],
            grad_w_fc1,
            early[4 * width : spot],
            grad_w_fc2,
            early[:width],
        )

    return body


def solution(mesh):
    return jax.shard_map(
        make_body(mesh.shape["dp"], mesh.shape["mp"]),
        mesh=mesh,
        in_specs=(
            P("dp", None),
            P("dp", None),
            P(),
            P(),
            P(None, None, "mp"),
            P(None, "mp"),
            P("mp", None),
            P(),
            P(),
            P(),
            P(None, "mp"),
            P("mp"),
            P("mp", None),
            P(),
            P("dp", None),
        ),
        out_specs=(
            P("dp", None),
            P("dp", None),
            P(),
            P(),
            P(None, None, "mp"),
            P(None, "mp"),
            P("mp", None),
            P(),
            P(),
            P(),
            P(None, "mp"),
            P("mp"),
            P("mp", None),
            P(),
        ),
        check_vma=False,
    )
```

time: 812 us -> 769 us (0.947)
  waiting for transfers between devices: 577 us -> 454 us
  starting transfers between devices: 0.59 us -> 80.7 us
  other arithmetic: 24 us -> 93.7 us
  blocking collectives: 65.4 us -> 0 us
  between operations: 14.6 us -> 2.92 us
    psum x4 -> x0, waiting for transfers between devices: 577 us -> none  [the longest x1 375 us: body(): lax.psum((grad_ln1_gain, grad_ln1_bias, grad_w_qkv, grad_b_qkv, grad_w_pr...]
    ppermute x0 -> x84, waiting for transfers between devices: none -> 454 us  [swap(): return lax.ppermute(value, axis, [(i, i ^ mask) for i in range(size)])]
    ppermute x0 -> x84, starting transfers between devices: none -> 80.7 us  [swap(): return lax.ppermute(value, axis, [(i, i ^ mask) for i in range(size)])]
    psum x1 -> x0, blocking collectives: 65.4 us -> none  [body(): lax.psum((grad_ln1_gain, grad_ln1_bias, grad_w_qkv, grad_b_qkv, grad_w_pr...]
    select_n x0 -> x35, other arithmetic: none -> 59 us  [double(): jnp.where(jnp.stack([first, ~first])[:, None, None], value[None], other[N...]
    unnamed x101 -> x166, local copies, waits for them, and re-layouts: 35.1 us -> 5.91 us
    broadcast_in_dim x0 -> x56, local copies, waits for them, and re-layouts: none -> 15.7 us  [double(): jnp.where(jnp.stack([first, ~first])[:, None, None], value[None], other[N...]
    reshape x1 -> x8, local copies, waits for them, and re-layouts: 2.54 us -> 17 us  [the longest x1 2.74 us: body(): grad_heads = dot_nt(grad_mid_low, w_proj).astype(BF16).reshape(shape)]
  transfers between devices with their start and end apart: 4 -> 84, of which waited for: 4 -> 37; matrix products, arithmetic and copies ran while one was open for 5% -> 20% of each run, Pallas kernels for 0% -> 0%
where the time goes in v1:
time: 769 us; the launch traced here: 758 us
  waiting for transfers between devices  454 us (59%)
  other arithmetic  93.7 us (12%)
  starting transfers between devices  80.7 us (10%)
  matrix products  70.5 us (9%)
  local copies, waits for them, and re-layouts  57 us (7%)
    ppermute x84, waiting for transfers between devices, swap(): return lax.ppermute(value, axis, [(i, i ^ mask) for i in range(size)])  454 us
    ppermute x84, starting transfers between devices, swap(): return lax.ppermute(value, axis, [(i, i ^ mask) for i in range(size)])  80.7 us
    select_n x35, other arithmetic, double(): jnp.where(jnp.stack([first, ~first])[:, None, None], value[None], other[N...  59 us
    dot_general x6, matrix products, dot_nt(): lax.dot_general(left, right, (((1,), (1,)), ((), ())), preferred_element_...  20.4 us
    dot_general x18, matrix products, dot_tn(): lax.dot_general(left, right, (((0,), (0,)), ((), ())), preferred_element_...  18.3 us
    dot_general x6, matrix products, dot_nn(): return jnp.dot(left, right, preferred_element_type=F32)  16.3 us
    broadcast_in_dim x56, local copies, waits for them, and re-layouts, double(): jnp.where(jnp.stack([first, ~first])[:, None, None], value[None], other[N...  15.7 us
  transfers between devices with their start and end apart: 84, of which 37 were waited for; matrix products, arithmetic and copies ran while one was open for 20% of the time, Pallas kernels for 0%

profile of v1, /device:TPU:0, one launch (start us, length us, event | category | flops | bytes accessed | tf_op | source)
XLA Modules:
  0.0 758.4 jit_solution(14305641394375694415)
XLA Ops:
  43.1 40.4 %collective-permute-done = f32[500,1024]{1,0:T(8,128)} collective-permute-done((f32[500,1024]{1,0:T(8,128)}, f32[500,1024]{1,0:T(8,128)}, u32[]{:S(2)}, u32[]{:S(2)}) %collective-permute-start) | collective-permute-done | bytes 2048032 | tf_op jit(solution)/shard_map/ppermute | solution.py:38
  90.9 12.6 %convert_reduce_fusion = (f32[2048]{0:T(1024)S(1)}, bf16[500,2048]{1,0:T(8,128)(2,1)S(1)}, f32[500,2048]{1,0:T(8,128)S(1)}) fusion(f32[500,2048]{1,0:T(8,128)S(1)} %fusion.113, f32[2048]{0:T(1024)S(1)} %copy-done.57, bf16[500,1024]{1,0:T(8,128)(2,1)S(1)} %copy-done.8, bf16[2048,1024]{1,0:T(8,128)(2,1)S(1)} %copy-done.74), kind=kOutput, calls=%fused_computation.8 | convolution fusion | flops 2173949952 | bytes 15474688 | tf_op jit(solution)/shard_map/dot_general | solution.py:20
  125.3 31.6 %collective-permute-done.2 = f32[500,1024]{1,0:T(8,128)S(1)} collective-permute-done((f32[500,1024]{1,0:T(8,128)S(1)}, f32[500,1024]{1,0:T(8,128)S(1)}, u32[]{:S(2)}, u32[]{:S(2)}) %collective-permute-start.2) | collective-permute-done | bytes 2048032 | tf_op jit(solution)/shard_map/ppermute | solution.py:38
  158.1 42.1 %collective-permute-done.1 = f32[500,1024]{1,0:T(8,128)S(1)} collective-permute-done((f32[500,1024]{1,0:T(8,128)S(1)}, f32[500,1024]{1,0:T(8,128)S(1)}, u32[]{:S(2)}, u32[]{:S(2)}) %collective-permute-start.1) | collective-permute-done | bytes 2048032 | tf_op jit(solution)/shard_map/ppermute | solution.py:38
  248.4 16.8 %collective-permute-done.33 = f32[64,512]{1,0:T(8,128)S(1)} collective-permute-done((f32[64,512]{1,0:T(8,128)S(1)}, f32[64,512]{1,0:T(8,128)S(1)}, u32[]{:S(2)}, u32[]{:S(2)}) %collective-permute-start.33) | collective-permute-done | bytes 131104 | tf_op jit(solution)/shard_map/ppermute | solution.py:38
  290.3 26.2 %collective-permute-done.37 = f32[32,512]{1,0:T(8,128)S(1)} collective-permute-done((f32[32,512]{1,0:T(8,128)S(1)}, f32[32,512]{1,0:T(8,128)S(1)}, u32[]{:S(2)}, u32[]{:S(2)}) %collective-permute-start.37) | collective-permute-done | bytes 65568 | tf_op jit(solution)/shard_map/ppermute | solution.py:38
  317.8 4.9 collective-permute-done.38
  340.8 7.3 collective-permute-done.25
  350.7 6.9 collective-permute-done.26
  370.0 4.9 collective-permute-done.17
  375.0 28.3 %collective-permute-done.9 = f32[256,512]{1,0:T(8,128)S(1)} collective-permute-done((f32[256,512]{1,0:T(8,128)S(1)}, f32[256,512]{1,0:T(8,128)S(1)}, u32[]{:S(2)}, u32[]{:S(2)}) %collective-permute-start.9) | collective-permute-done | bytes 524320 | tf_op jit(solution)/shard_map/ppermute | solution.py:38
  418.2 14.5 %collective-permute-done.69 = f32[320,1024]{1,0:T(8,128)S(1)} collective-permute-done((f32[320,1024]{1,0:T(8,128)S(1)}, f32[320,1024]{1,0:T(8,128)S(1)}, u32[]{:S(2)}, u32[]{:S(2)}) %collective-permute-start.69) | collective-permute-done | bytes 1310752 | tf_op jit(solution)/shard_map/ppermute | solution.py:38
  437.4 15.3 %collective-permute-done.54 = f32[80,2048]{1,0:T(8,128)S(1)} collective-permute-done((f32[80,2048]{1,0:T(8,128)S(1)}, f32[80,2048]{1,0:T(8,128)S(1)}, u32[]{:S(2)}, u32[]{:S(2)}) %collective-permute-start.54) | collective-permute-done | bytes 655392 | tf_op jit(solution)/shard_map/ppermute | solution.py:38
  453.1 12.7 %collective-permute-done.70 = f32[160,1024]{1,0:T(8,128)S(1)} collective-permute-done((f32[160,1024]{1,0:T(8,128)S(1)}, f32[160,1024]{1,0:T(8,128)S(1)}, u32[]{:S(2)}, u32[]{:S(2)}) %collective-permute-start.70) | collective-permute-done | bytes 655392 | tf_op jit(solution)/shard_map/ppermute | solution.py:38
  466.1 16.3 %collective-permute-done.55 = f32[40,2048]{1,0:T(8,128)S(1)} collective-permute-done((f32[40,2048]{1,0:T(8,128)S(1)}, f32[40,2048]{1,0:T(8,128)S(1)}, u32[]{:S(2)}, u32[]{:S(2)}) %collective-permute-start.55) | collective-permute-done | bytes 327712 | tf_op jit(solution)/shard_map/ppermute | solution.py:38
  482.4 16.9 %collective-permute-done.71 = f32[80,1024]{1,0:T(8,128)S(1)} collective-permute-done((f32[80,1024]{1,0:T(8,128)S(1)}, f32[80,1024]{1,0:T(8,128)S(1)}, u32[]{:S(2)}, u32[]{:S(2)}) %collective-permute-start.71) | collective-permute-done | bytes 327712 | tf_op jit(solution)/shard_map/ppermute | solution.py:38
  506.1 25.0 %collective-permute-done.56 = f32[40,2048]{1,0:T(8,128)S(1)} collective-permute-done((f32[40,2048]{1,0:T(8,128)S(1)}, f32[40,2048]{1,0:T(8,128)S(1)}, u32[]{:S(2)}, u32[]{:S(2)}) %collective-permute-start.56) | collective-permute-done | bytes 327712 | tf_op jit(solution)/shard_map/ppermute | solution.py:38
  531.3 9.6 %collective-permute-done.72 = f32[80,1024]{1,0:T(8,128)S(1)} collective-permute-done((f32[80,1024]{1,0:T(8,128)S(1)}, f32[80,1024]{1,0:T(8,128)S(1)}, u32[]{:S(2)}, u32[]{:S(2)}) %collective-permute-start.72) | collective-permute-done | bytes 327712 | tf_op jit(solution)/shard_map/ppermute | solution.py:38
  544.8 7.4 collective-permute-done.47
  555.4 13.8 %collective-permute-done.6 = f32[16,128]{1,0:T(8,128)S(1)} collective-permute-done((f32[16,128]{1,0:T(8,128)S(1)}, f32[16,128]{1,0:T(8,128)S(1)}, u32[]{:S(2)}, u32[]{:S(2)}) %collective-permute-start.6) | collective-permute-done | bytes 8224 | tf_op jit(solution)/shard_map/ppermute | solution.py:38
  570.5 8.9 %collective-permute-done.48 = f32[32,1024]{1,0:T(8,128)S(1)} collective-permute-done((f32[32,1024]{1,0:T(8,128)S(1)}, f32[32,1024]{1,0:T(8,128)S(1)}, u32[]{:S(2)}, u32[]{:S(2)}) %collective-permute-start.48) | collective-permute-done | bytes 131104 | tf_op jit(solution)/shard_map/ppermute | solution.py:38
  606.6 31.7 %collective-permute-done.12 = f32[64,512]{1,0:T(8,128)S(1)} collective-permute-done((f32[64,512]{1,0:T(8,128)S(1)}, f32[64,512]{1,0:T(8,128)S(1)}, u32[]{:S(2)}, u32[]{:S(2)}) %collective-permute-start.12) | collective-permute-done | bytes 131104 | tf_op jit(solution)/shard_map/ppermute | solution.py:38
  644.2 31.9 %collective-permute-done.30 = f32[192,512]{1,0:T(8,128)S(1)} collective-permute-done((f32[192,512]{1,0:T(8,128)S(1)}, f32[192,512]{1,0:T(8,128)S(1)}, u32[]{:S(2)}, u32[]{:S(2)}) %collective-permute-start.30) | collective-permute-done | bytes 393248 | tf_op jit(solution)/shard_map/ppermute | solution.py:38
  753.0 5.1 pad_maximum_fusion.1
  (554 shorter events, 324.3 us)
Async XLA Ops:
  35.4 48.2 %collective-permute-start = (f32[500,1024]{1,0:T(8,128)}, f32[500,1024]{1,0:T(8,128)}, u32[]{:S(2)}, u32[]{:S(2)}) collective-permute-start(f32[500,1024]{1,0:T(8,128)} %fusion.112), channel_id=1, source_target_pairs={{0,1},{1,0},{2,3},{3,2},{4,5},{5,4},{6,7},{7,6},{8,9},{9,8},{10,11... | collective-permute-start | bytes 6144008 | tf_op jit(solution)/shard_map/ppermute | solution.py:38
  109.1 47.8 %collective-permute-start.2 = (f32[500,1024]{1,0:T(8,128)S(1)}, f32[500,1024]{1,0:T(8,128)S(1)}, u32[]{:S(2)}, u32[]{:S(2)}) collective-permute-start(f32[500,1024]{1,0:T(8,128)S(1)} %fusion.115), channel_id=1, source_target_pairs={{0,1},{1,0},{2,3},{3,2},{4,5},{5,4},{6,7},{7,6},{8,9},{9,8},{10,11... | collective-permute-start | bytes 6144008 | tf_op jit(solution)/shard_map/ppermute | solution.py:38
  113.3 87.0 %collective-permute-start.1 = (f32[500,1024]{1,0:T(8,128)S(1)}, f32[500,1024]{1,0:T(8,128)S(1)}, u32[]{:S(2)}, u32[]{:S(2)}) collective-permute-start(f32[500,1024]{1,0:T(8,128)S(1)} %fusion.114), channel_id=1, source_target_pairs={{0,1},{1,0},{2,3},{3,2},{4,5},{5,4},{6,7},{7,6},{8,9},{9,8},{10,11... | collective-permute-start | bytes 6144008 | tf_op jit(solution)/shard_map/ppermute | solution.py:38
  116.8 164.8 %collective-permute-start.52 = (f32[320,2048]{1,0:T(8,128)}, f32[320,2048]{1,0:T(8,128)}, u32[]{:S(2)}, u32[]{:S(2)}) collective-permute-start(f32[320,2048]{1,0:T(8,128)} %fusion.59), channel_id=1, source_target_pairs={{0,2},{2,0},{4,6},{6,4},{8,10},{10,8},{12,14},{14,12},{16,18},{18,... | collective-permute-start | bytes 7864328 | tf_op jit(solution)/shard_map/ppermute | solution.py:38
  119.3 166.9 %collective-permute-start.68 = (f32[640,1024]{1,0:T(8,128)}, f32[640,1024]{1,0:T(8,128)}, u32[]{:S(2)}, u32[]{:S(2)}) collective-permute-start(f32[640,1024]{1,0:T(8,128)} %fusion.45), channel_id=1, source_target_pairs={{0,2},{2,0},{4,6},{6,4},{8,10},{10,8},{12,14},{14,12},{16,18},{18,... | collective-permute-start | bytes 7864328 | tf_op jit(solution)/shard_map/ppermute | solution.py:38
  121.6 125.2 %collective-permute-start.61 = (f32[96,2048]{1,0:T(8,128)}, f32[96,2048]{1,0:T(8,128)}, u32[]{:S(2)}, u32[]{:S(2)}) collective-permute-start(f32[96,2048]{1,0:T(8,128)} %constant_dynamic-slice_fusion.8), channel_id=1, source_target_pairs={{0,8},{2,10},{4,12},{6,14},{8,0},{10,2},{12,4},{14,6},{16,24},{18,... | collective-permute-start | bytes 2359304 | tf_op jit(solution)/shard_map/ppermute | solution.py:38
  246.4 91.2 %collective-permute-start.44 = (f32[256,1024]{1,0:T(8,128)S(1)}, f32[256,1024]{1,0:T(8,128)S(1)}, u32[]{:S(2)}, u32[]{:S(2)}) collective-permute-start(f32[256,1024]{1,0:T(8,128)S(1)} %copy-done.34), channel_id=1, source_target_pairs={{0,2},{2,0},{4,6},{6,4},{8,10},{10,8},{12,14},{14,12},{16,18},{18,... | collective-permute-start | bytes 3145736 | tf_op jit(solution)/shard_map/ppermute | solution.py:38
  265.1 59.3 %collective-permute-start.24 = (f32[384,512]{1,0:T(8,128)S(1)}, f32[384,512]{1,0:T(8,128)S(1)}, u32[]{:S(2)}, u32[]{:S(2)}) collective-permute-start(f32[384,512]{1,0:T(8,128)S(1)} %fusion.62), channel_id=1, source_target_pairs={{0,2},{2,0},{4,6},{6,4},{8,10},{10,8},{12,14},{14,12},{16,18},{18,... | collective-permute-start | bytes 2359304 | tf_op jit(solution)/shard_map/ppermute | solution.py:38
  322.7 111.4 %collective-permute-start.3 = (f32[500,1024]{1,0:T(8,128)S(1)}, f32[500,1024]{1,0:T(8,128)S(1)}, u32[]{:S(2)}, u32[]{:S(2)}) collective-permute-start(f32[500,1024]{1,0:T(8,128)S(1)} %add_add_fusion), channel_id=1, source_target_pairs={{0,1},{1,0},{2,3},{3,2},{4,5},{5,4},{6,7},{7,6},{8,9},{9,8},{10,11... | collective-permute-start | bytes 6144008 | tf_op jit(solution)/shard_map/ppermute | solution.py:38
  359.9 57.6 %collective-permute-start.53 = (f32[160,2048]{1,0:T(8,128)S(1)}, f32[160,2048]{1,0:T(8,128)S(1)}, u32[]{:S(2)}, u32[]{:S(2)}) collective-permute-start(f32[160,2048]{1,0:T(8,128)S(1)} %constant_dynamic-slice_fusion.11), channel_id=1, source_target_pairs={{0,4},{2,6},{4,0},{6,2},{8,12},{10,14},{12,8},{14,10},{16,20},{18,... | collective-permute-start | bytes 3932168 | tf_op jit(solution)/shard_map/ppermute | solution.py:38
  414.8 87.6 %collective-permute-start.43 = (f32[56,128]{1,0:T(8,128)S(1)}, f32[56,128]{1,0:T(8,128)S(1)}, u32[]{:S(2)}, u32[]{:S(2)}) collective-permute-start(f32[56,128]{1,0:T(8,128)S(1)} %add.531), channel_id=1, source_target_pairs={{0,16},{2,18},{4,20},{6,22},{8,24},{10,26},{12,28},{14,30},{16,0},... | collective-permute-start | bytes 86024 | tf_op jit(solution)/shard_map/ppermute | solution.py:38
  417.5 125.2 %collective-permute-start.39 = (f32[128,512]{1,0:T(8,128)S(1)}, f32[128,512]{1,0:T(8,128)S(1)}, u32[]{:S(2)}, u32[]{:S(2)}) collective-permute-start(f32[128,512]{1,0:T(8,128)S(1)} %bitcast_select_fusion.30), channel_id=1, source_target_pairs={{0,2},{2,0},{4,6},{6,4},{8,10},{10,8},{12,14},{14,12},{16,18},{18,... | collective-permute-start | bytes 786440 | tf_op jit(solution)/shard_map/ppermute | solution.py:38
  417.5 125.3 %collective-permute-start.81 = (f32[96,1024]{1,0:T(8,128)S(1)}, f32[96,1024]{1,0:T(8,128)S(1)}, u32[]{:S(2)}, u32[]{:S(2)}) collective-permute-start(f32[96,1024]{1,0:T(8,128)S(1)} %bitcast_select_fusion.26), channel_id=1, source_target_pairs={{0,16},{2,18},{4,20},{6,22},{8,24},{10,26},{12,28},{14,30},{16,0},... | collective-permute-start | bytes 1179656 | tf_op jit(solution)/shard_map/ppermute | solution.py:38
  452.8 46.6 %collective-permute-start.4 = (f32[16,128]{1,0:T(8,128)S(1)}, f32[16,128]{1,0:T(8,128)S(1)}, u32[]{:S(2)}, u32[]{:S(2)}) collective-permute-start(f32[16,128]{1,0:T(8,128)S(1)} %pad_maximum_fusion.3), channel_id=1, source_target_pairs={{0,2},{2,0},{4,6},{6,4},{8,10},{10,8},{12,14},{14,12},{16,18},{18,... | collective-permute-start | bytes 24584 | tf_op jit(solution)/shard_map/ppermute | solution.py:38
  499.4 41.6 %collective-permute-start.72 = (f32[80,1024]{1,0:T(8,128)S(1)}, f32[80,1024]{1,0:T(8,128)S(1)}, u32[]{:S(2)}, u32[]{:S(2)}) collective-permute-start(f32[80,1024]{1,0:T(8,128)S(1)} %dynamic-slice_add_fusion.12), channel_id=1, source_target_pairs={{0,16},{2,18},{4,20},{6,22},{8,24},{10,26},{12,28},{14,30},{16,0},... | collective-permute-start | bytes 983048 | tf_op jit(solution)/shard_map/ppermute | solution.py:38
  506.1 46.2 %collective-permute-start.65 = (f32[48,2048]{1,0:T(8,128)S(1)}, f32[48,2048]{1,0:T(8,128)S(1)}, u32[]{:S(2)}, u32[]{:S(2)}) collective-permute-start(f32[48,2048]{1,0:T(8,128)S(1)} %bitcast_select_fusion.27), channel_id=1, source_target_pairs={{0,16},{2,18},{4,20},{6,22},{8,24},{10,26},{12,28},{14,30},{16,0},... | collective-permute-start | bytes 1179656 | tf_op jit(solution)/shard_map/ppermute | solution.py:38
  552.2 48.6 %collective-permute-start.73 = (f32[160,1024]{1,0:T(8,128)}, f32[160,1024]{1,0:T(8,128)}, u32[]{:S(2)}, u32[]{:S(2)}) collective-permute-start(f32[160,1024]{1,0:T(8,128)} %bitcast_select_fusion.20), channel_id=1, source_target_pairs={{0,8},{2,10},{4,12},{6,14},{8,0},{10,2},{12,4},{14,6},{16,24},{18,... | collective-permute-start | bytes 1966088 | tf_op jit(solution)/shard_map/ppermute | solution.py:38
  552.3 44.1 %collective-permute-start.29 = (f32[96,512]{1,0:T(8,128)}, f32[96,512]{1,0:T(8,128)}, u32[]{:S(2)}, u32[]{:S(2)}) collective-permute-start(f32[96,512]{1,0:T(8,128)} %bitcast_select_fusion.33), channel_id=1, source_target_pairs={{0,8},{2,10},{4,12},{6,14},{8,0},{10,2},{12,4},{14,6},{16,24},{18,... | collective-permute-start | bytes 589832 | tf_op jit(solution)/shard_map/ppermute | solution.py:38
  554.4 42.1 %collective-permute-start.11 = (f32[64,512]{1,0:T(8,128)}, f32[64,512]{1,0:T(8,128)}, u32[]{:S(2)}, u32[]{:S(2)}) collective-permute-start(f32[64,512]{1,0:T(8,128)} %constant_dynamic-slice_fusion.24), channel_id=1, source_target_pairs={{0,16},{2,18},{4,20},{6,22},{8,24},{10,26},{12,28},{14,30},{16,0},... | collective-permute-start | bytes 393224 | tf_op jit(solution)/shard_map/ppermute | solution.py:38
  596.3 87.7 %collective-permute-start.82 = (f32[192,1024]{1,0:T(8,128)}, f32[192,1024]{1,0:T(8,128)}, u32[]{:S(2)}, u32[]{:S(2)}) collective-permute-start(f32[192,1024]{1,0:T(8,128)} %bitcast_select_fusion.17), channel_id=1, source_target_pairs={{0,8},{2,10},{4,12},{6,14},{8,0},{10,2},{12,4},{14,6},{16,24},{18,... | collective-permute-start | bytes 2359304 | tf_op jit(solution)/shard_map/ppermute | solution.py:38
  596.4 90.7 %collective-permute-start.66 = (f32[96,2048]{1,0:T(8,128)}, f32[96,2048]{1,0:T(8,128)}, u32[]{:S(2)}, u32[]{:S(2)}) collective-permute-start(f32[96,2048]{1,0:T(8,128)} %bitcast_select_fusion.18), channel_id=1, source_target_pairs={{0,8},{2,10},{4,12},{6,14},{8,0},{10,2},{12,4},{14,6},{16,24},{18,... | collective-permute-start | bytes 2359304 | tf_op jit(solution)/shard_map/ppermute | solution.py:38
  598.4 42.9 %collective-permute-start.49 = (f32[64,1024]{1,0:T(8,128)}, f32[64,1024]{1,0:T(8,128)}, u32[]{:S(2)}, u32[]{:S(2)}) collective-permute-start(f32[64,1024]{1,0:T(8,128)} %bitcast_select_fusion.29), channel_id=1, source_target_pairs={{0,8},{2,10},{4,12},{6,14},{8,0},{10,2},{12,4},{14,6},{16,24},{18,... | collective-permute-start | bytes 786440 | tf_op jit(solution)/shard_map/ppermute | solution.py:38
  598.5 103.6 %collective-permute-start.58 = (f32[160,2048]{1,0:T(8,128)}, f32[160,2048]{1,0:T(8,128)}, u32[]{:S(2)}, u32[]{:S(2)}) collective-permute-start(f32[160,2048]{1,0:T(8,128)} %bitcast_select_fusion.13), channel_id=1, source_target_pairs={{0,4},{2,6},{4,0},{6,2},{8,12},{10,14},{12,8},{14,10},{16,20},{18,... | collective-permute-start | bytes 3932168 | tf_op jit(solution)/shard_map/ppermute | solution.py:38
  638.3 68.9 %collective-permute-start.74 = (f32[320,1024]{1,0:T(8,128)}, f32[320,1024]{1,0:T(8,128)}, u32[]{:S(2)}, u32[]{:S(2)}) collective-permute-start(f32[320,1024]{1,0:T(8,128)} %bitcast_select_fusion.12), channel_id=1, source_target_pairs={{0,4},{2,6},{4,0},{6,2},{8,12},{10,14},{12,8},{14,10},{16,20},{18,... | collective-permute-start | bytes 3932168 | tf_op jit(solution)/shard_map/ppermute | solution.py:38
  (140 other events, 3463.6 us)

commit v2 on v1

v2 whole, which is shorter than its diff:
```python
import functools

import jax
import jax.numpy as jnp
from jax import lax
from jax.experimental import pallas as pl
from jax.experimental.pallas import tpu as pltpu
from jax.sharding import PartitionSpec as P

HEAD = 64
BF16 = jnp.bfloat16
MESH = pl.DeviceIdType.MESH
F32 = jnp.float32


def dot_nn(left, right):
    return jnp.dot(left, right, preferred_element_type=F32)


def dot_tn(left, right):
    return lax.dot_general(left, right, (((0,), (0,)), ((), ())), preferred_element_type=F32)


def dot_nt(left, right):
    return lax.dot_general(left, right, (((1,), (1,)), ((), ())), preferred_element_type=F32)


def norm_parts(value):
    centered = value - jnp.mean(value, axis=-1, keepdims=True)
    variance = jnp.mean(centered * centered, axis=-1, keepdims=True)
    inverse = lax.rsqrt(variance + 1e-06)
    return centered * inverse, inverse


def norm_back(grad, normalized, inverse, gain):
    scaled = grad * gain
    mean_one = jnp.mean(scaled, axis=-1, keepdims=True)
    mean_two = jnp.mean(scaled * normalized, axis=-1, keepdims=True)
    return inverse * (scaled - mean_one - normalized * mean_two)


def swap(value, axis, size, mask):
    return lax.ppermute(value, axis, [(i, i ^ mask) for i in range(size)])


def plan(shapes, unit_bytes=1 << 20):
    out = []
    for rows, cols in shapes:
        count = max(1, rows * cols * 4 // 2 // unit_bytes)
        out.append((rows // 2 // count, cols, count))
    return out


def add_into(dst, src_a, src_b, rows):
    step = 16

    @pl.loop(0, rows // step)
    def _(i):
        at = pl.ds(pl.multiple_of(i * step, step), step)
        dst[at, :] = src_a[at, :] + src_b[at, :]


def sum_kernel(layout, offs, n_arr, *refs):
    ins = refs[:n_arr]
    outs = refs[n_arr : 2 * n_arr]
    rest = refs[2 * n_arr :]
    per = 10
    bufs = [rest[i * per : (i + 1) * per] for i in range(n_arr)]
    send_sem, recv_sem, load_sem, out_sem, away_sem, land_sem = rest[n_arr * per :]
    me, mp = lax.axis_index("dp"), lax.axis_index("mp")
    core, y, z = me % 2, (me // 2) % 2, me // 4
    to_core = (me + 1 - 2 * core, mp)
    to_y = (me + 2 - 4 * y, mp)
    to_z = (me + 4 - 8 * (z % 2), mp)
    to_mid = (me + 4 - 8 * ((z + 1) % 2), mp)
    center = z * (3 - z) > 0
    leaf = z * (3 - z) == 0
    upper = z // 2

    barrier = pltpu.get_barrier_semaphore()
    for target in (to_core, to_y, to_z):
        pl.semaphore_signal(barrier, inc=1, device_id=target, device_id_type=MESH)

    @pl.when(center)
    def _():
        pl.semaphore_signal(barrier, inc=1, device_id=to_mid, device_id_type=MESH)
        pl.semaphore_wait(barrier, 4)

    @pl.when(leaf)
    def _():
        pl.semaphore_wait(barrier, 3)

    def remote(src, dst, unit, stage, target):
        return pltpu.make_async_remote_copy(
            src_ref=src, dst_ref=dst, send_sem=send_sem.at[unit, stage], recv_sem=recv_sem.at[unit, stage],
            device_id=target, device_id_type=MESH,
        )

    actions = []
    finals = []
    unit_id = 0
    first = []
    order = []
    for a, (m, cols, count) in enumerate(layout):
        for j in range(count):
            order.append((a, j, 0))
            order.append((a, j, 1))
    p_seen = r_seen = 0
    for a, j, kind in order:
        m, cols, count = layout[a]
        n, h = m // 2, m // 4
        acc, got, y_in, z_in, m_in, a_in, rz_in, rm_in, ry_in, ra_in = bufs[a]
        g, o = ins[a], outs[a]
        base = (kind * count + j) * m
        slot = kind * count + j
        u = unit_id
        unit_id += 1
        mine = base + core * n
        theirs = base + (1 - core) * n
        acc_u = acc.at[slot]
        rows_at = lambda start, size: pl.ds(pl.multiple_of(start, 8), size)
        load = pltpu.make_async_copy(g.at[rows_at(mine, n), :], acc_u, load_sem.at[u])
        swap = remote(g.at[rows_at(theirs, n), :], got.at[slot], u, 0, to_core)
        first.append((load, swap))

        def start_sum(load=load, swap=swap, acc_u=acc_u, got_u=got.at[slot], n=n):
            load.wait()
            swap.wait_recv()
            add_into(acc_u, acc_u, got_u, n)

        def emit(src, at, size, idx, u=u, o=o):
            here = pltpu.make_async_copy(src, o.at[rows_at(at, size), :], out_sem.at[u, idx])
            there = pltpu.make_async_remote_copy(
                src_ref=src, dst_ref=o.at[rows_at(at, size), :], send_sem=away_sem.at[u, idx],
                recv_sem=land_sem.at[u, idx], device_id=to_core, device_id_type=MESH,
            )
            here.start()
            there.start()

            def end():
                here.wait()
                there.wait()

            return end

        if kind == 0:
            t0 = p_seen * offs["slot"]
            p_seen += 1
            keep, away = rows_at(y * h, h), rows_at((1 - y) * h, h)
            acc_k, acc_w = acc_u.at[keep], acc_u.at[away]
            ys = remote(acc_w, y_in.at[j], u, 1, to_y)
            up = remote(acc_k, z_in.at[j], u, 2, to_z)
            md = remote(acc_k, m_in.at[j], u, 3, to_mid)
            dn = remote(m_in.at[j], z_in.at[j], u, 4, to_z)
            ag_c = remote(m_in.at[j], a_in.at[j], u, 5, to_y)
            ag_l = remote(z_in.at[j], a_in.at[j], u, 5, to_y)

            def s0(start_sum=start_sum, ys=ys):
                start_sum()
                ys.start()

            def s1(ys=ys, up=up, acc_k=acc_k, y_u=y_in.at[j], h=h):
                ys.wait_recv()
                add_into(acc_k, acc_k, y_u, h)

                @pl.when(leaf)
                def _():
                    up.start()

            def s2(up=up, md=md, acc_k=acc_k, z_u=z_in.at[j], h=h):
                @pl.when(center)
                def _():
                    up.wait_recv()
                    add_into(acc_k, acc_k, z_u, h)
                    md.start()

            def s3(md=md, dn=dn, ag_c=ag_c, acc_k=acc_k, m_u=m_in.at[j], h=h):
                @pl.when(center)
                def _():
                    md.wait_recv()
                    add_into(m_u, acc_k, m_u, h)
                    dn.start()
                    ag_c.start()

            def s4(dn=dn, ag_l=ag_l):
                @pl.when(leaf)
                def _():
                    dn.wait_recv()
                    ag_l.start()

            def s5(dn=dn, up=up, md=md, ag_c=ag_c, ag_l=ag_l, ys=ys, swap=swap, mine=mine, h=h, j=j, m_in=m_in,
                   z_in=z_in, a_in=a_in, emit=emit):
                ag_c.wait_recv()
                end_a = emit(a_in.at[j], mine + (1 - y) * h, h, 1)

                @pl.when(center)
                def _():
                    emit(m_in.at[j], mine + y * h, h, 0)

                @pl.when(leaf)
                def _():
                    emit(z_in.at[j], mine + y * h, h, 0)

                def end():
                    end_a()
                    src = m_in.at[j]
                    o = outs_of
                    swap.wait_send()
                    ys.wait_send()
                    ag_c.wait_send()

                    @pl.when(leaf)
                    def _():
                        up.wait_send()

                    @pl.when(center)
                    def _():
                        md.wait_send()
                        dn.wait_send()

                outs_of = None
                return end

            def wait_final(u=u, o=o, m_in=m_in, j=j, mine=mine, h=h):
                pltpu.make_async_copy(m_in.at[j], o.at[rows_at(mine + y * h, h), :], out_sem.at[u, 0]).wait()
                pltpu.make_async_remote_copy(
                    src_ref=m_in.at[j], dst_ref=o.at[rows_at(mine + y * h, h), :], send_sem=away_sem.at[u, 0],
                    recv_sem=land_sem.at[u, 0], device_id=to_core, device_id_type=MESH,
                ).wait()

            for k, s in enumerate((s0, s1, s2, s3, s4)):
                actions.append((t0 + offs["p"][k], len(actions), s))

            def s5w(s5=s5, wait_final=wait_final):
                end = s5()
                finals.append(end)
                finals.append(wait_final)

            actions.append((t0 + offs["p"][5], len(actions), s5w))
        else:
            t0 = r_seen * offs["slot"] + offs["lag"]
            r_seen += 1
            own, oth = rows_at(upper * h, h), rows_at((1 - upper) * h, h)
            acc_o, acc_t = acc_u.at[own], acc_u.at[oth]
            up = remote(acc_u, rz_in.at[j], u, 1, to_z)
            md = remote(acc_t, rm_in.at[j], u, 2, to_mid)
            ys = remote(acc_o, ry_in.at[j], u, 3, to_y)
            ma = remote(ry_in.at[j], ra_in.at[j], u, 4, to_mid)
            d0 = remote(ry_in.at[j], rz_in.at[j].at[own], u, 5, to_z)
            d1 = remote(ra_in.at[j], rz_in.at[j].at[oth], u, 6, to_z)

            def s0(start_sum=start_sum, up=up):
                start_sum()

                @pl.when(leaf)
                def _():
                    up.start()

            def s1(up=up, md=md, acc_u=acc_u, z_u=rz_in.at[j], n=n):
                @pl.when(center)
                def _():
                    up.wait_recv()
                    add_into(acc_u, acc_u, z_u, n)
                    md.start()

            def s2(md=md, ys=ys, acc_o=acc_o, m_u=rm_in.at[j], h=h):
                @pl.when(center)
                def _():
                    md.wait_recv()
                    add_into(acc_o, acc_o, m_u, h)
                    ys.start()

            def s3(ys=ys, ma=ma, d0=d0, acc_o=acc_o, y_u=ry_in.at[j], h=h, emit=emit, mine=mine):
                @pl.when(center)
                def _():
                    ys.wait_recv()
                    add_into(y_u, acc_o, y_u, h)
                    ma.start()
                    d0.start()
                    emit(y_u, mine + upper * h, h, 0)

            def s4(ma=ma, d1=d1, ra_u=ra_in.at[j], emit=emit, mine=mine, h=h):
                @pl.when(center)
                def _():
                    ma.wait_recv()
                    d1.start()
                    emit(ra_u, mine + (1 - upper) * h, h, 1)

            def s5(d0=d0, d1=d1, z_u=rz_in.at[j], emit=emit, mine=mine, h=h, own=own, oth=oth):
                @pl.when(leaf)
                def _():
                    d0.wait_recv()
                    emit(z_u.at[own], mine + upper * h, h, 0)
                    d1.wait_recv()
                    emit(z_u.at[oth], mine + (1 - upper) * h, h, 1)

            def s6(u=u, o=o, z_u=rz_in.at[j], mine=mine, h=h, swap=swap, up=up, md=md, ys=ys, ma=ma, d0=d0, d1=d1,
                   own=own, oth=oth):
                for idx, part, at in ((0, own, upper * h), (1, oth, (1 - upper) * h)):
                    pltpu.make_async_copy(z_u.at[part], o.at[rows_at(mine + at, h), :], out_sem.at[u, idx]).wait()
                    pltpu.make_async_remote_copy(
                        src_ref=z_u.at[part], dst_ref=o.at[rows_at(mine + at, h), :], send_sem=away_sem.at[u, idx],
                        recv_sem=land_sem.at[u, idx], device_id=to_core, device_id_type=MESH,
                    ).wait()
                swap.wait_send()

                @pl.when(leaf)
                def _():
                    up.wait_send()

                @pl.when(center)
                def _():
                    for c in (md, ys, ma, d0, d1):
                        c.wait_send()

            for k, s in enumerate((s0, s1, s2, s3, s4, s5)):
                actions.append((t0 + offs["r"][k], len(actions), s))
            finals.append(s6)

    for load, swap in first:
        load.start()
        swap.start()
    for _, _, act in sorted(actions, key=lambda t: t[:2]):
        act()
    for end in finals:
        end()


OFFS = {"slot": 1.0, "lag": 0.2, "p": (0, 1, 2, 3, 4, 5), "r": (0, 1.3, 2, 2.7, 3.4, 4.5)}


def sum_dp(arrays, offs=OFFS, unit_bytes=1 << 20):
    layout = plan([a.shape for a in arrays], unit_bytes)
    scratch = []
    units = 0
    for m, cols, count in layout:
        n, h = m // 2, m // 4
        units += 2 * count
        for c, r in ((2 * count, n), (2 * count, n), (count, h), (count, h), (count, h), (count, h),
                     (count, n), (count, h), (count, h), (count, h)):
            scratch.append(pltpu.VMEM((c, r, cols), F32))
    scratch += [
        pltpu.SemaphoreType.DMA((units, 7)), pltpu.SemaphoreType.DMA((units, 7)), pltpu.SemaphoreType.DMA((units,)),
        pltpu.SemaphoreType.DMA((units, 2)), pltpu.SemaphoreType.DMA((units, 2)), pltpu.SemaphoreType.DMA((units, 2)),
    ]
    anyspec = pl.BlockSpec(memory_space=pl.ANY)
    return pl.pallas_call(
        functools.partial(sum_kernel, layout, offs, len(arrays)),
        out_shape=[jax.ShapeDtypeStruct(a.shape, F32) for a in arrays],
        in_specs=[anyspec] * len(arrays),
        out_specs=[anyspec] * len(arrays),
        scratch_shapes=scratch,
        name="sum_dp",
        compiler_params=pltpu.CompilerParams(collective_id=0, has_side_effects=True, vmem_limit_bytes=62 << 20),
    )(*arrays)


def small_kernel(value_ref, out_ref, got, send_sem, recv_sem):
    me, mp = lax.axis_index("dp"), lax.axis_index("mp")
    core, y, z = me % 2, (me // 2) % 2, me // 4
    targets = (
        me + 1 - 2 * core,
        me + 2 - 4 * y,
        me + 4 - 8 * (z % 2),
        me + 8 - 16 * (z // 2),
    )
    barrier = pltpu.get_barrier_semaphore()
    for target in targets:
        pl.semaphore_signal(barrier, inc=1, device_id=(target, mp), device_id_type=MESH)
    pl.semaphore_wait(barrier, 4)
    out_ref[...] = value_ref[...]
    src = value_ref
    for k, target in enumerate(targets):
        copy = pltpu.make_async_remote_copy(
            src_ref=src, dst_ref=got.at[k], send_sem=send_sem.at[k], recv_sem=recv_sem.at[k],
            device_id=(target, mp), device_id_type=MESH,
        )
        copy.start()
        copy.wait()
        if k < 3:
            got[4 + k] = src[...] + got[k]
            src = got.at[4 + k]
        else:
            out_ref[...] = src[...] + got[k]


def sum_dp_small(value):
    return pl.pallas_call(
        small_kernel,
        out_shape=jax.ShapeDtypeStruct(value.shape, F32),
        in_specs=[pl.BlockSpec(memory_space=pltpu.VMEM)],
        out_specs=pl.BlockSpec(memory_space=pltpu.VMEM),
        scratch_shapes=[
            pltpu.VMEM((7,) + value.shape, F32),
            pltpu.SemaphoreType.DMA((4,)),
            pltpu.SemaphoreType.DMA((4,)),
        ],
        name="sum_dp_small",
        compiler_params=pltpu.CompilerParams(collective_id=1, has_side_effects=True),
    )(value)


def make_body(n_dp, n_mp):
    fast = n_dp == 16 and n_mp == 2

    def sum_mp(part):
        if n_mp == 2:
            return part + swap(part, "mp", 2, 1)
        return lax.psum(part, "mp")

    def body(
        tokens, keep_mask, ln1_gain, ln1_bias, w_qkv, b_qkv, w_proj, b_proj,
        ln2_gain, ln2_bias, w_fc1, b_fc1, w_fc2, b_fc2, cotangent,
    ):
        inputs = tokens.astype(F32)
        tok_rows, width = inputs.shape
        images = keep_mask.shape[0]
        slots = tok_rows // images
        cols = w_qkv.shape[2]
        heads = cols // HEAD
        shape = (images, slots, heads, HEAD)

        normal_one, inverse_one = norm_parts(inputs)
        norm_one = (normal_one * ln1_gain + ln1_bias).astype(BF16)
        weight = w_qkv.transpose(1, 0, 2)
        query = (dot_nn(norm_one, weight[0]) + b_qkv[0]).astype(BF16).reshape(shape)
        keys = dot_nn(norm_one, weight[1]).astype(BF16).reshape(shape)
        values = (dot_nn(norm_one, weight[2]) + b_qkv[1]).astype(BF16).reshape(shape)
        scores = jnp.einsum("bqhd,bkhd->bhqk", query, keys, preferred_element_type=F32) * 0.125
        live = (keep_mask > 0)[:, None, None, :]
        masked = jnp.where(live, scores, -1e30)
        row_max = jnp.max(masked, axis=-1, keepdims=True)
        exp_terms = jnp.where(live, jnp.exp(masked - row_max), 0.0)
        probs = exp_terms / jnp.sum(exp_terms, axis=-1, keepdims=True)
        probs_low = probs.astype(BF16)
        mixed = jnp.einsum("bhqk,bkhd->bqhd", probs_low, values, preferred_element_type=F32)
        heads_out = mixed.reshape(tok_rows, cols).astype(BF16)
        after_attn = inputs + sum_mp(dot_nn(heads_out, w_proj)) + b_proj

        normal_two, inverse_two = norm_parts(after_attn)
        norm_two = (normal_two * ln2_gain + ln2_bias).astype(BF16)
        pre_act = dot_nn(norm_two, w_fc1) + b_fc1
        hidden_f, gelu_back = jax.vjp(lambda v: jax.nn.gelu(v, approximate=False), pre_act)
        hidden = hidden_f.astype(BF16)
        grad_w_fc2 = dot_tn(hidden, cotangent)
        grad_pre = gelu_back(dot_nt(cotangent, w_fc2))[0].astype(BF16)
        grad_norm_two = sum_mp(dot_nt(grad_pre, w_fc1))
        grad_w_fc1 = dot_tn(norm_two, grad_pre)
        mlp_sum = sum_mp(dot_nn(hidden, w_fc2))
        layer_out = (after_attn + mlp_sum + b_fc2).astype(BF16)

        grad_out = cotangent.astype(F32)
        grad_mid = grad_out + norm_back(grad_norm_two, normal_two, inverse_two, ln2_gain)
        grad_mid_low = grad_mid.astype(BF16)
        grad_heads = dot_nt(grad_mid_low, w_proj).astype(BF16).reshape(shape)
        grad_w_proj = dot_tn(heads_out, grad_mid_low)
        grad_probs = jnp.einsum("bqhd,bkhd->bhqk", grad_heads, values, preferred_element_type=F32)
        grad_values = jnp.einsum(
            "bhqk,bqhd->bkhd", probs_low, grad_heads, preferred_element_type=F32
        ).astype(BF16)
        inner = jnp.sum(probs * grad_probs, axis=-1, keepdims=True)
        grad_scores = (probs * (grad_probs - inner)).astype(BF16)
        grad_query = (
            jnp.einsum("bhqk,bkhd->bqhd", grad_scores, keys, preferred_element_type=F32) * 0.125
        ).astype(BF16)
        grad_keys = (
            jnp.einsum("bhqk,bqhd->bkhd", grad_scores, query, preferred_element_type=F32) * 0.125
        ).astype(BF16)
        grad_query = grad_query.reshape(tok_rows, cols)
        grad_keys = grad_keys.reshape(tok_rows, cols)
        grad_values = grad_values.reshape(tok_rows, cols)
        part = (
            dot_nt(grad_query, weight[0])
            + dot_nt(grad_keys, weight[1])
            + dot_nt(grad_values, weight[2])
        )
        grad_norm_one = sum_mp(part)
        grads = [
            grad_w_fc2,
            grad_w_fc1,
            grad_w_proj,
            dot_tn(norm_one, grad_values),
            dot_tn(norm_one, grad_query),
            dot_tn(norm_one, grad_keys),
        ]
        if fast:
            grads = sum_dp(grads)
        else:
            grads = lax.psum(grads, "dp")
        grad_w_fc2, grad_w_fc1, grad_w_proj, grad_w_v, grad_w_q, grad_w_k = grads
        grad_w_qkv = jnp.stack([grad_w_q, grad_w_k, grad_w_v], axis=1)
        grad_tokens = (
            grad_mid + norm_back(grad_norm_one, normal_one, inverse_one, ln1_gain)
        ).astype(BF16)

        small = jnp.concatenate(
            [
                jnp.sum(grad_out, axis=0),
                jnp.sum(grad_norm_two * normal_two, axis=0),
                jnp.sum(grad_norm_two, axis=0),
                jnp.sum(grad_mid, axis=0),
                jnp.sum(grad_norm_one * normal_one, axis=0),
                jnp.sum(grad_norm_one, axis=0),
                jnp.sum(grad_pre.astype(F32), axis=0),
                jnp.sum(grad_query.astype(F32), axis=0),
                jnp.sum(grad_values.astype(F32), axis=0),
            ]
        )
        if fast:
            small = sum_dp_small(small.reshape(-1, 128)).reshape(-1)
        else:
            small = lax.psum(small, "dp")
        rows = [small[k * width : (k + 1) * width] for k in range(6)]
        spot = 6 * width + b_fc1.shape[0]
        return (
            layer_out,
            grad_tokens,
            rows[4],
            rows[5],
            grad_w_qkv,
            small[spot:].reshape(2, cols),
            grad_w_proj,
            rows[3],
            rows[1],
            rows[2],
            grad_w_fc1,
            small[6 * width : spot],
            grad_w_fc2,
            rows[0],
        )

    return body


def solution(mesh):
    return jax.shard_map(
        make_body(mesh.shape["dp"], mesh.shape["mp"]),
        mesh=mesh,
        in_specs=(
            P("dp", None),
            P("dp", None),
            P(),
            P(),
            P(None, None, "mp"),
            P(None, "mp"),
            P("mp", None),
            P(),
            P(),
            P(),
            P(None, "mp"),
            P("mp"),
            P("mp", None),
            P(),
            P("dp", None),
        ),
        out_specs=(
            P("dp", None),
            P("dp", None),
            P(),
            P(),
            P(None, None, "mp"),
            P(None, "mp"),
            P("mp", None),
            P(),
            P(),
            P(),
            P(None, "mp"),
            P("mp"),
            P("mp", None),
            P(),
        ),
        check_vma=False,
    )
```

time: 769 us -> 542 us (0.70)
  waiting for transfers between devices: 454 us -> 122 us
  Pallas kernels: 0 us -> 267 us
  starting transfers between devices: 80.7 us -> 6.58 us
  other arithmetic: 93.7 us -> 24.3 us
  local copies, waits for them, and re-layouts: 57 us -> 39.7 us
    ppermute x84 -> x4, waiting for transfers between devices: 454 us -> 122 us  [swap(): return lax.ppermute(value, axis, [(i, i ^ mask) for i in range(size)])]
    pallas_call x0 -> x2, Pallas kernels: none -> 267 us  [the longest x1 254 us: sum_dp(): pl.pallas_call(functools.partial(sum_kernel, layout, offs, len(arrays)),...]
    ppermute x84 -> x4, starting transfers between devices: 80.7 us -> 6.58 us  [swap(): return lax.ppermute(value, axis, [(i, i ^ mask) for i in range(size)])]
    select_n x35 -> x0, other arithmetic: 59 us -> none  [double(): jnp.where(jnp.stack([first, ~first])[:, None, None], value[None], other[N...]
    broadcast_in_dim x56 -> x0, local copies, waits for them, and re-layouts: 15.7 us -> none  [double(): jnp.where(jnp.stack([first, ~first])[:, None, None], value[None], other[N...]
    unnamed x166 -> x79, local copies, waits for them, and re-layouts: 5.91 us -> 18.1 us
    concatenate x3 -> x0, other arithmetic: 9.57 us -> none  [the longest x2 9.57 us: sum_outer(): return jnp.concatenate(total, axis=0) if len(total) > 1 else total[0]]
    dot_general x18 -> x6, matrix products: 18.3 us -> 21.5 us  [dot_tn(): lax.dot_general(left, right, (((0,), (0,)), ((), ())), preferred_element_...]
  transfers between devices with their start and end apart: 84 -> 4, of which waited for: 37 -> 3; matrix products, arithmetic and copies ran while one was open for 20% -> 6% of each run, Pallas kernels for 0% -> 48%
where the time goes in v2:
time: 542 us; the launch traced here: 533 us
  Pallas kernels  267 us (49%)
  waiting for transfers between devices  122 us (23%)
  matrix products  71.3 us (13%)
  local copies, waits for them, and re-layouts  39.7 us (7%)
  other arithmetic  24.3 us (4%)
  starting transfers between devices  6.58 us (1%)
    pallas_call x1, Pallas kernels, sum_dp(): pl.pallas_call(functools.partial(sum_kernel, layout, offs, len(arrays)),...  254 us
    ppermute x4, waiting for transfers between devices, swap(): return lax.ppermute(value, axis, [(i, i ^ mask) for i in range(size)])  122 us
    dot_general x6, matrix products, dot_tn(): lax.dot_general(left, right, (((0,), (0,)), ((), ())), preferred_element_...  21.5 us
    dot_general x6, matrix products, dot_nt(): lax.dot_general(left, right, (((1,), (1,)), ((), ())), preferred_element_...  21.5 us
    unnamed x79, local copies, waits for them, and re-layouts  18.1 us
    dot_general x6, matrix products, dot_nn(): return jnp.dot(left, right, preferred_element_type=F32)  13.8 us
    pallas_call x1, Pallas kernels, sum_dp_small(): pl.pallas_call(small_kernel, out_shape=jax.ShapeDtypeStruct(value.shape,...  13 us
  transfers between devices with their start and end apart: 4, of which 3 were waited for; matrix products, arithmetic and copies ran while one was open for 6% of the time, Pallas kernels for 48%

profile of v2, /device:TPU:0, one launch (start us, length us, event | category | flops | bytes accessed | tf_op | source)
XLA Modules:
  0.0 533.3 jit_solution(5112726686064857342)
XLA Ops:
  6.9 3.0 fusion.28
  12.2 3.0 fusion.29
  19.1 4.4 fusion.68
  23.5 2.8 fusion.26
  30.0 3.0 collective-permute-start
  33.0 44.9 %collective-permute-done = f32[500,1024]{1,0:T(8,128)S(1)} collective-permute-done((f32[500,1024]{1,0:T(8,128)S(1)}, f32[500,1024]{1,0:T(8,128)S(1)}, u32[]{:S(2)}, u32[]{:S(2)}) %collective-permute-start) | collective-permute-done | bytes 2048032 | tf_op jit(solution)/shard_map/ppermute | solution.py:43
  80.1 2.6 fusion.53
  82.7 12.5 %convert_reduce_fusion = (f32[2048]{0:T(1024)S(1)}, bf16[500,2048]{1,0:T(8,128)(2,1)S(1)}, f32[500,2048]{1,0:T(8,128)S(1)}) fusion(f32[500,2048]{1,0:T(8,128)S(1)} %fusion.53, f32[2048]{0:T(1024)S(1)} %copy-done.24, bf16[500,1024]{1,0:T(8,128)(2,1)S(1)} %copy-done.16, bf16[2048,1024]{1,0:T(8,128)(2,1)S(1)} %copy-done.29), kind=kOutput, calls=%fused_computation.4 | convolution fusion | flops 2173949952 | bytes 15474688 | tf_op jit(solution)/shard_map/dot_general | solution.py:25
  103.2 6.1 %fusion.52.refs_1_ = f32[1024,2048]{1,0:T(8,128)} fusion(bf16[500,2048]{1,0:T(8,128)(2,1)S(1)} %get-tuple-element.35, f32[500,1024]{1,0:T(8,128)S(1)} %get-tuple-element.42, f32[1024]{0:T(1024)S(1)} %copy-done.30, f32[1024]{0:T(1024)S(1)} %copy-done.22, f32[500]{0:T(512)S(1)} %add_rsqrt_fusion, f32[500]{0:T(512)S(1)} %broadcast_multiply_fusion.4), kind=kOutput, calls=%fused_computation.122 | convolution fusion | flops 2099712000 | bytes 12496800 | tf_op jit(solution)/shard_map/dot_general | solution.py:21
  109.3 36.3 %collective-permute-done.2 = f32[500,1024]{1,0:T(8,128)S(1)} collective-permute-done((f32[500,1024]{1,0:T(8,128)S(1)}, f32[500,1024]{1,0:T(8,128)S(1)}, u32[]{:S(2)}, u32[]{:S(2)}) %collective-permute-start.2) | collective-permute-done | bytes 2048032 | tf_op jit(solution)/shard_map/ppermute | solution.py:43
  146.8 41.2 %collective-permute-done.1 = f32[500,1024]{1,0:T(8,128)S(1)} collective-permute-done((f32[500,1024]{1,0:T(8,128)S(1)}, f32[500,1024]{1,0:T(8,128)S(1)}, u32[]{:S(2)}, u32[]{:S(2)}) %collective-permute-start.1) | collective-permute-done | bytes 2048032 | tf_op jit(solution)/shard_map/ppermute | solution.py:43
  193.2 2.6 reshape.123
  195.8 3.9 convert_reduce_fusion.3
  218.2 5.8 %fusion.80.refs_0_ = f32[2048,1024]{1,0:T(8,128)} fusion(bf16[500,2048]{1,0:T(8,128)(2,1)S(1)} %copy-done.15, bf16[500,1024]{1,0:T(8,128)(2,1)S(1)} %copy-done.17), kind=kOutput, calls=%fused_computation.134 | convolution fusion | flops 2097152000 | bytes 11460608 | tf_op jit(solution)/shard_map/dot_general | solution.py:21
  224.1 2.4 fusion.56.refs_4_
  226.6 2.4 fusion.58.refs_3_
  229.0 2.7 fusion.54.refs_5_
  233.7 254.4 %sum_dp.1 = (f32[2048,1024]{1,0:T(8,128)}, f32[1024,2048]{1,0:T(8,128)}, f32[512,1024]{1,0:T(8,128)}, f32[1024,512]{1,0:T(8,128)}, f32[1024,512]{1,0:T(8,128)}, /*index=5*/f32[1024,512]{1,0:T(8,128)}) custom-call(f32[2048,1024]{1,0:T(8,128)} %fusion.80.refs_0_, f32[1024,2048]{1,0:T(8,128)} %fusion.52.refs_1_, f32[512,1024]{1,0:T(8,128)} %fusion.47.refs_2_, ...), custom_call_target="tpu_custom_call" | custom-call | tf_op jit(solution)/shard_map/sum_dp/pallas_call | solution.py:347
  488.2 6.4 %pad_maximum_fusion = f32[1024,3,512]{2,0,1:T(8,128)} fusion(f32[1024,1,512]{2,0,1:T(8,128)} %bitcast.79, f32[1024,1,512]{2,0,1:T(8,128)} %bitcast.81, f32[1024,1,512]{2,0,1:T(8,128)} %bitcast.80), kind=kLoop, calls=%fused_computation.1 | loop fusion | flops 3145728 | bytes 12582912 | tf_op jit(solution)/shard_map/stack | solution.py:491
  494.5 4.6 fusion.20
  499.8 13.0 %sum_dp_small.1 = f32[72,128]{1,0:T(8,128)} custom-call(f32[72,128]{1,0:T(8,128)} %bitcast.82), custom_call_target="tpu_custom_call" | custom-call | tf_op jit(solution)/shard_map/sum_dp_small/pallas_call | solution.py:388
  516.1 3.4 fusion.19
  520.8 8.6 %copy.99 = f32[1024,2048]{1,0:T(8,128)} copy(f32[1024,2048]{1,0:T(8,128)} %get-tuple-element.88) | data formatting | bytes 16777216
  529.4 3.4 copy.100
  (128 shorter events, 58.4 us)
Async XLA Ops:
  0.6 28.6 %copy-start = (bf16[512,1024]{1,0:T(8,128)(2,1)S(1)}, bf16[512,1024]{1,0:T(8,128)(2,1)}, u32[]{:S(2)}) copy-start(bf16[512,1024]{1,0:T(8,128)(2,1)} %param.21) | copy-start | bytes 3145732
  0.7 4.0 copy-start.5
  0.7 4.0 copy-start.27
  0.7 4.0 copy-start.23
  0.7 4.0 copy-start.31
  29.3 48.6 %copy-start.25 = (f32[1024]{0:T(1024)S(1)}, f32[1024]{0:T(1024)}, u32[]{:S(2)}) copy-start(f32[1024]{0:T(1024)} %param.22) | copy-start | bytes 12292
  30.0 47.9 %collective-permute-start = (f32[500,1024]{1,0:T(8,128)S(1)}, f32[500,1024]{1,0:T(8,128)S(1)}, u32[]{:S(2)}, u32[]{:S(2)}) collective-permute-start(f32[500,1024]{1,0:T(8,128)S(1)} %fusion.77), channel_id=1, source_target_pairs={{0,1},{1,0},{2,3},{3,2},{4,5},{5,4},{6,7},{7,6},{8,9},{9,8},{10,11... | collective-permute-start | bytes 6144008 | tf_op jit(solution)/shard_map/ppermute | solution.py:43
  97.6 47.9 %collective-permute-start.2 = (f32[500,1024]{1,0:T(8,128)S(1)}, f32[500,1024]{1,0:T(8,128)S(1)}, u32[]{:S(2)}, u32[]{:S(2)}) collective-permute-start(f32[500,1024]{1,0:T(8,128)S(1)} %fusion.79), channel_id=1, source_target_pairs={{0,1},{1,0},{2,3},{3,2},{4,5},{5,4},{6,7},{7,6},{8,9},{9,8},{10,11... | collective-permute-start | bytes 6144008 | tf_op jit(solution)/shard_map/ppermute | solution.py:43
  102.8 85.2 %collective-permute-start.1 = (f32[500,1024]{1,0:T(8,128)S(1)}, f32[500,1024]{1,0:T(8,128)S(1)}, u32[]{:S(2)}, u32[]{:S(2)}) collective-permute-start(f32[500,1024]{1,0:T(8,128)S(1)} %fusion.78), channel_id=1, source_target_pairs={{0,1},{1,0},{2,3},{3,2},{4,5},{5,4},{6,7},{7,6},{8,9},{9,8},{10,11... | collective-permute-start | bytes 6144008 | tf_op jit(solution)/shard_map/ppermute | solution.py:43
  109.3 78.8 %copy-start.26 = (f32[1024]{0:T(1024)S(1)}, f32[1024]{0:T(1024)}, u32[]{:S(2)}) copy-start(f32[1024]{0:T(1024)} %param.28) | copy-start | bytes 12292
  195.7 3.9 copy-start.9
  195.7 3.9 copy-start.19
  195.7 3.9 copy-start.20
  214.7 3.5 copy-start.15
  214.7 3.5 copy-start.17
  216.7 7.4 %copy-start.11 = (bf16[500,512]{1,0:T(8,128)(2,1)S(1)}, bf16[500,512]{1,0:T(8,128)(2,1)}, u32[]{:S(2)}) copy-start(bf16[500,512]{1,0:T(8,128)(2,1)} %reshape.124) | copy-start | bytes 1536004
  216.7 277.8 %collective-permute-start.3 = (f32[500,1024]{1,0:T(8,128)}, f32[500,1024]{1,0:T(8,128)}, u32[]{:S(2)}, u32[]{:S(2)}) collective-permute-start(f32[500,1024]{1,0:T(8,128)} %add_add_fusion), channel_id=1, source_target_pairs={{0,1},{1,0},{2,3},{3,2},{4,5},{5,4},{6,7},{7,6},{8,9},{9,8},{10,11... | collective-permute-start | bytes 6144008 | tf_op jit(solution)/shard_map/ppermute | solution.py:43
  229.0 2.7 copy-start.3
  488.2 6.4 %copy-start.6 = (bf16[500,1024]{1,0:T(8,128)(2,1)S(1)}, bf16[500,1024]{1,0:T(8,128)(2,1)}, u32[]{:S(2)}) copy-start(bf16[500,1024]{1,0:T(8,128)(2,1)} %param.15) | copy-start | bytes 3072004
  494.5 21.6 %copy-start.4 = (f32[500,1024]{1,0:T(8,128)S(1)}, f32[500,1024]{1,0:T(8,128)}, u32[]{:S(2)}) copy-start(f32[500,1024]{1,0:T(8,128)} %copy-done.2) | copy-start | bytes 6144004
  516.1 3.4 copy-start.10
  519.5 9.9 %slice-start = ((s8[8388608]{0:T(1024)(128)(4,1)}), s8[4194304]{0:T(1024)(128)(4,1)S(1)}, s32[]{:S(2)}) async-start(s8[8388608]{0:T(1024)(128)(4,1)} %bitcast.71), calls=%async_computation | async-start | bytes 8388608
  520.8 8.6 %slice-start.1 = ((s8[8388608]{0:T(1024)(128)(4,1)}), s8[4194304]{0:T(1024)(128)(4,1)S(1)}, s32[]{:S(2)}) async-start(s8[8388608]{0:T(1024)(128)(4,1)} %bitcast.71), calls=%async_computation.1 | async-start | bytes 8388608
  529.4 3.4 copy-start.1
  (14 other events, 26.0 us)

commit v3 on v1

v3 whole, which is shorter than its diff:
```python
import functools

import jax
import jax.numpy as jnp
from jax import lax
from jax.experimental import pallas as pl
from jax.experimental.pallas import tpu as pltpu
from jax.sharding import PartitionSpec as P

HEAD = 64
BF16 = jnp.bfloat16
MESH = pl.DeviceIdType.MESH
F32 = jnp.float32


def dot_nn(left, right):
    return jnp.dot(left, right, preferred_element_type=F32)


def dot_tn(left, right):
    return lax.dot_general(left, right, (((0,), (0,)), ((), ())), preferred_element_type=F32)


def dot_nt(left, right):
    return lax.dot_general(left, right, (((1,), (1,)), ((), ())), preferred_element_type=F32)


def norm_parts(value):
    centered = value - jnp.mean(value, axis=-1, keepdims=True)
    variance = jnp.mean(centered * centered, axis=-1, keepdims=True)
    inverse = lax.rsqrt(variance + 1e-06)
    return centered * inverse, inverse


def norm_back(grad, normalized, inverse, gain):
    scaled = grad * gain
    mean_one = jnp.mean(scaled, axis=-1, keepdims=True)
    mean_two = jnp.mean(scaled * normalized, axis=-1, keepdims=True)
    return inverse * (scaled - mean_one - normalized * mean_two)


def swap(value, axis, size, mask):
    return lax.ppermute(value, axis, [(i, i ^ mask) for i in range(size)])


def split_plan(shapes, unit_bytes=1 << 20):
    out = []
    for rows, cols in shapes:
        count = max(1, rows * cols * 4 // 2 // unit_bytes)
        out.append((rows // 2 // count, cols, count))
    return out


def rows_at(start, size):
    return pl.ds(pl.multiple_of(start, 8), size)


def each_block(total, step, body, carry=()):
    full = total // step
    if full:
        carry = lax.fori_loop(
            0, full, lambda i, c: body(pl.ds(pl.multiple_of(i * step, step), step), c), carry
        )
    if total % step:
        carry = body(pl.ds(full * step, total % step), carry)
    return carry


def add_into(dst, src_a, src_b):
    @pl.loop(0, dst.shape[0] // 16)
    def _(i):
        at = pl.ds(pl.multiple_of(i * 16, 16), 16)
        dst[at, :] = src_a[at, :] + src_b[at, :]


def fold(value):
    return jnp.sum(value, axis=0, keepdims=True)


def norm_back_rows(value, grad, gain):
    normal, inverse = norm_parts(value)
    return normal, norm_back(grad, normal, inverse, gain)


def attend_back(q, k, v, g, live, first):
    grad_q = grad_k = grad_v = None
    for own in (first, 1 - first):
        own = own.astype(BF16)
        q_own, g_own, k_own = q * own, g * own, k * own
        scores = jnp.where(live, dot_nt(q_own, k) * 0.125, -1e30)
        exp_terms = jnp.where(live, jnp.exp(scores - jnp.max(scores, axis=-1, keepdims=True)), 0.0)
        probs = exp_terms / jnp.maximum(jnp.sum(exp_terms, axis=-1, keepdims=True), 1.0)
        grad_probs = dot_nt(g_own, v)
        inner = jnp.sum(probs * grad_probs, axis=-1, keepdims=True)
        grad_scores = (probs * (grad_probs - inner)).astype(BF16)
        parts = (dot_nn(grad_scores, k_own), dot_tn(grad_scores, q_own), dot_tn(probs.astype(BF16), g_own))
        if grad_q is None:
            grad_q, grad_k, grad_v = parts
        else:
            grad_q, grad_k, grad_v = grad_q + parts[0], grad_k + parts[1], grad_v + parts[2]
    return (grad_q * 0.125).astype(BF16), (grad_k * 0.125).astype(BF16), grad_v.astype(BF16)


BUFFERS = 7


def back_kernel(layout, keys, slots, group, *refs):
    (g_fc2, g_fc1, near_hbm, mlp_hbm, after_hbm, tok_hbm, cot_hbm, q_hbm, k_hbm, v_hbm, live_hbm, wproj_hbm,
     wqkv_hbm, n1t_hbm, ht_hbm, vec_hbm) = refs[:16]
    o_fc2, o_fc1, o_v, o_proj, o_q, o_k, o_layer, o_tok, o_small = refs[16:25]
    rest = refs[25:]
    bufs = [rest[i * BUFFERS : (i + 1) * BUFFERS] for i in range(6)]
    (near, far, far_one, after, mid, low, g_heads, q_s, k_s, v_s, g_proj, wproj, wqkv, n1t, ht, cot, tok, live_s,
     vec, small, small_in, st_fc2, st_fc1, st_qkv,
     free_sem, send_sem, recv_sem, out_sem, away_sem, land_sem, in_sem, st_sem, x_send, x_recv, v_send, v_recv, fin_sem,
     ) = rest[6 * BUFFERS :]
    ins = (g_fc2, g_fc1, None, None, None, None)
    outs = (o_fc2, o_fc1, o_v, o_proj, o_q, o_k)
    stage = (st_fc2, st_fc1, st_qkv, st_fc2, st_qkv, st_qkv)

    me, mp = lax.axis_index("dp"), lax.axis_index("mp")
    core, y, z = me % 2, (me // 2) % 2, me // 4
    to_core = (me + 1 - 2 * core, mp)
    to_y = (me + 2 - 4 * y, mp)
    to_z = (me + 4 - 8 * (z % 2), mp)
    to_mid = (me + 4 - 8 * ((z + 1) % 2), mp)
    to_far = (me + 8 - 16 * (z // 2), mp)
    to_x = (me, 1 - mp)
    centre = z * (3 - z) > 0
    leaf = z * (3 - z) == 0
    upper = z // 2
    tok_rows = near_hbm.shape[0]

    loads = [
        pltpu.make_async_copy(src, dst, in_sem.at[i])
        for i, (src, dst) in enumerate((
            (near_hbm, near), (after_hbm, after), (cot_hbm, cot), (vec_hbm, vec),
            (wproj_hbm, wproj), (q_hbm, q_s), (k_hbm, k_s), (v_hbm, v_s), (live_hbm, live_s), (ht_hbm, ht),
            (n1t_hbm, n1t), (wqkv_hbm, wqkv), (tok_hbm, tok),
        ))
    ]
    for load in loads[:4]:
        load.start()

    barrier = pltpu.get_barrier_semaphore()
    for target in (to_core, to_y, to_z, to_x, to_far):
        pl.semaphore_signal(barrier, inc=1, device_id=target, device_id_type=MESH)

    @pl.when(centre)
    def _():
        pl.semaphore_signal(barrier, inc=1, device_id=to_mid, device_id_type=MESH)
        pl.semaphore_wait(barrier, 6)

    @pl.when(leaf)
    def _():
        pl.semaphore_wait(barrier, 5)

    def copy_x(src, dst, index):
        return pltpu.make_async_remote_copy(
            src_ref=src, dst_ref=dst, send_sem=x_send.at[index], recv_sem=x_recv.at[index],
            device_id=to_x, device_id_type=MESH,
        )

    swap_two = copy_x(near_hbm, far, 0)
    swap_one = copy_x(near, far_one, 1)
    swap_mlp = copy_x(mlp_hbm, far, 2)
    swap_two.start()

    def remote(src, dst, unit, step, target):
        return pltpu.make_async_remote_copy(
            src_ref=src, dst_ref=dst, send_sem=send_sem.at[unit, step], recv_sem=recv_sem.at[unit, step],
            device_id=target, device_id_type=MESH,
        )

    actions = []
    ends = []

    def act(key):
        def keep(fn):
            actions.append((key, len(actions), fn))
            return fn

        return keep

    def both_outputs(src, out, at, size, unit, index):
        place = out.at[rows_at(at, size), :]
        here = pltpu.make_async_copy(src, place, out_sem.at[unit, index])
        there = pltpu.make_async_remote_copy(
            src_ref=src, dst_ref=place, send_sem=away_sem.at[unit, index], recv_sem=land_sem.at[unit, index],
            device_id=to_core, device_id_type=MESH,
        )
        return here, there

    def emit(*args):
        for copy in both_outputs(*args):
            copy.start()

    def product(a, start, size):
        if a == 3:
            return dot_nn(ht[rows_at(start, size), :], low[...])
        return dot_nn(n1t[rows_at(start, size), :], g_proj[{2: 2, 4: 0, 5: 1}[a]])

    unit = 0
    for a, (m, cols, count) in enumerate(layout):
        made = ins[a] is None
        for kind, j in [(kind, j) for j in range(count) for kind in (0, 1)]:
            n, h = m // 2, m // 4
            acc = bufs[a][0].at[kind * count + j]
            y_in, z_in, m_in, rz_in, rm_in, ry_in = (ref.at[j] for ref in bufs[a][1:])
            out = outs[a]
            base = (kind * count + j) * m
            mine, theirs = base + core * n, base + (1 - core) * n
            seq = j * 2 + kind
            t0 = slots[a][j] + (keys["lag"] if kind else 0.0)
            u = unit
            unit += 1
            spare = stage[a].at[seq % 2]
            if not made:
                swap = remote(ins[a].at[rows_at(theirs, n), :], acc, u, 0, to_core)
                load = lambda s, a=a, n=n, m=m, count=count: pltpu.make_async_copy(
                    ins[a].at[rows_at(((s % 2) * count + s // 2) * m + core * n, n), :],
                    stage[a].at[s % 2], st_sem.at[a, s % 2])

                @act(-2.0 + 0.01 * u)
                def _(swap=swap, load=load, seq=seq):
                    swap.start()
                    if seq < 2:
                        load(seq).start()

                def gather(swap=swap, load=load, seq=seq, acc=acc, spare=spare, count=count):
                    load(seq).wait()
                    swap.wait_recv()
                    add_into(acc, acc, spare)
                    if seq + 2 < 2 * count:
                        load(seq + 2).start()
            else:
                swap = remote(spare, acc, u, 0, to_core)

                @act(t0 - keys["ahead"])
                def _(swap=swap, spare=spare, a=a, theirs=theirs, n=n):
                    spare[...] = product(a, theirs, n)
                    swap.start()

                def gather(swap=swap, acc=acc, a=a, mine=mine, n=n):
                    own = product(a, mine, n)
                    swap.wait_recv()
                    acc[...] = acc[...] + own
                    swap.wait_send()

            if kind == 0:
                kept, away = acc.at[rows_at(y * h, h)], acc.at[rows_at((1 - y) * h, h)]
                over = remote(away, y_in, u, 1, to_y)
                up = remote(kept, z_in, u, 2, to_z)
                across = remote(kept, m_in, u, 3, to_mid)
                down = remote(m_in, z_in, u, 4, to_z)
                back_c = remote(m_in, kept, u, 5, to_y)
                back_l = remote(z_in, kept, u, 5, to_y)
                at_kept, at_away = mine + y * h, mine + (1 - y) * h

                @act(t0 + keys["p"][0])
                def _(gather=gather, over=over):
                    gather()
                    over.start()

                @act(t0 + keys["p"][1])
                def _(over=over, up=up, kept=kept, y_in=y_in, u=u):
                    over.wait_recv()
                    add_into(kept, kept, y_in)
                    over.wait_send()
                    pl.semaphore_signal(free_sem.at[u], inc=1, device_id=to_y, device_id_type=MESH)

                    @pl.when(leaf)
                    def _():
                        up.start()

                @act(t0 + keys["p"][2])
                def _(up=up, across=across, kept=kept, z_in=z_in):
                    @pl.when(centre)
                    def _():
                        up.wait_recv()
                        add_into(kept, kept, z_in)
                        across.start()

                @act(t0 + keys["p"][3])
                def _(over=over, across=across, down=down, back_c=back_c, kept=kept, m_in=m_in, out=out,
                      at_kept=at_kept, h=h, u=u):
                    @pl.when(centre)
                    def _():
                        across.wait_recv()
                        add_into(m_in, kept, m_in)
                        down.start()
                        pl.semaphore_wait(free_sem.at[u], 1)
                        back_c.start()
                        emit(m_in, out, at_kept, h, u, 0)

                @act(t0 + keys["p"][4])
                def _(down=down, back_l=back_l, z_in=z_in, out=out, at_kept=at_kept, h=h, u=u):
                    @pl.when(leaf)
                    def _():
                        down.wait_recv()
                        pl.semaphore_wait(free_sem.at[u], 1)
                        back_l.start()
                        emit(z_in, out, at_kept, h, u, 0)

                @act(t0 + keys["p"][5])
                def _(over=over, back_c=back_c, away=away, out=out, at_away=at_away, h=h, u=u):
                    back_c.wait_recv()
                    emit(away, out, at_away, h, u, 1)

                def end(swap=swap, made=made, up=up, across=across, down=down, back_c=back_c, m_in=m_in, away=away,
                        out=out, at_kept=at_kept, at_away=at_away, h=h, u=u):
                    for args in ((m_in, out, at_kept, h, u, 0), (away, out, at_away, h, u, 1)):
                        for copy in both_outputs(*args):
                            copy.wait()
                    if not made:
                        swap.wait_send()
                    back_c.wait_send()

                    @pl.when(leaf)
                    def _():
                        up.wait_send()

                    @pl.when(centre)
                    def _():
                        across.wait_send()
                        down.wait_send()
            else:
                at_own, at_other = upper * h, (1 - upper) * h
                own, other = rows_at(at_own, h), rows_at(at_other, h)
                up = remote(acc, rz_in, u, 1, to_z)
                across = remote(acc.at[other], rm_in, u, 2, to_mid)
                over = remote(acc.at[own], ry_in, u, 3, to_y)
                back = remote(ry_in, acc.at[own], u, 4, to_mid)
                down_a = remote(ry_in, rz_in.at[own], u, 5, to_z)
                down_b = remote(acc.at[other], rz_in.at[other], u, 6, to_z)
                emit_own = (out, mine + at_own, h, u, 0)
                emit_other = (out, mine + at_other, h, u, 1)

                @act(t0 + keys["r"][0])
                def _(gather=gather, up=up):
                    gather()

                    @pl.when(leaf)
                    def _():
                        up.start()

                @act(t0 + keys["r"][1])
                def _(up=up, across=across, acc=acc, rz_in=rz_in):
                    @pl.when(centre)
                    def _():
                        up.wait_recv()
                        add_into(acc, acc, rz_in)
                        across.start()

                @act(t0 + keys["r"][2])
                def _(across=across, over=over, acc=acc, own=own, rm_in=rm_in, u=u):
                    @pl.when(centre)
                    def _():
                        across.wait_recv()
                        add_into(acc.at[own], acc.at[own], rm_in)
                        over.start()
                        across.wait_send()
                        pl.semaphore_signal(free_sem.at[u], inc=1, device_id=to_mid, device_id_type=MESH)

                @act(t0 + keys["r"][3])
                def _(over=over, back=back, down_a=down_a, acc=acc, own=own, ry_in=ry_in, emit_own=emit_own, u=u):
                    @pl.when(centre)
                    def _():
                        over.wait_recv()
                        add_into(ry_in, acc.at[own], ry_in)
                        down_a.start()
                        pl.semaphore_wait(free_sem.at[u], 1)
                        back.start()
                        emit(ry_in, *emit_own)

                @act(t0 + keys["r"][4])
                def _(across=across, back=back, down_b=down_b, acc=acc, other=other, emit_other=emit_other):
                    @pl.when(centre)
                    def _():
                        back.wait_recv()
                        down_b.start()
                        emit(acc.at[other], *emit_other)

                @act(t0 + keys["r"][5])
                def _(down_a=down_a, down_b=down_b, rz_in=rz_in, own=own, other=other, emit_own=emit_own,
                      emit_other=emit_other):
                    @pl.when(leaf)
                    def _():
                        down_a.wait_recv()
                        emit(rz_in.at[own], *emit_own)
                        down_b.wait_recv()
                        emit(rz_in.at[other], *emit_other)

                def end(swap=swap, made=made, up=up, over=over, back=back, down_a=down_a, down_b=down_b, ry_in=ry_in,
                        emit_own=emit_own, emit_other=emit_other):
                    for args in (emit_own, emit_other):
                        for copy in both_outputs(ry_in, *args):
                            copy.wait()
                    if not made:
                        swap.wait_send()

                    @pl.when(leaf)
                    def _():
                        up.wait_send()

                    @pl.when(centre)
                    def _():
                        for copy in (over, back, down_a, down_b):
                            copy.wait_send()

            ends.append(end)

    @act(-1.0)
    def _():
        for load in loads[4:]:
            load.start()

    @act(keys["two"])
    def _():
        for load in loads[:4]:
            load.wait()
        swap_two.wait_recv()
        gain = vec[0:1, :]
        low[pl.ds(tok_rows // 16 * 16, 16), :] = jnp.zeros((16, low.shape[1]), BF16)

        def block(at, carry):
            grad = near[at, :] + far[at, :]
            normal, through = norm_back_rows(after[at, :], grad, gain)
            g_mid = cot[at, :].astype(F32) + through
            mid[at, :] = g_mid
            low[at, :] = g_mid.astype(BF16)
            return tuple(c + fold(v) for c, v in zip(carry, (grad * normal, grad, g_mid)))

        zero = jnp.zeros((1, low.shape[1]), F32)
        sums = each_block(tok_rows, 16, block, (zero, zero, zero))
        small[...] = vec[...]
        for k in range(3):
            small[k + 1 : k + 2, :] = sums[k]

    @act(keys["two"] + 0.001)
    def _():
        loads[4].wait()

        @pl.loop(0, 2)
        def _(i):
            at = pl.ds(pl.multiple_of(i * 256, 256), 256)
            g_heads[at, :] = dot_nt(low[at, :], wproj[...]).astype(BF16)

        for load in loads[5:9]:
            load.wait()

    starts = list(range(0, tok_rows, group))
    lanes = lax.broadcasted_iota(jnp.int32, (1, 128), 1)
    for i, start in enumerate(starts):
        stop = starts[i + 1] if i + 1 < len(starts) else q_s.shape[0]

        @act(keys["attn"][i])
        def _(start=start, size=stop - start):
            rows = pl.ds(start, size)
            first = (lanes < HEAD).astype(F32)

            @pl.loop(0, q_s.shape[1] // 128)
            def _(pair):
                cols = pl.ds(pl.multiple_of(pair * 128, 128), 128)
                live = live_s[rows, pl.ds(0, size)] > 0.0
                grads = attend_back(q_s[rows, cols], k_s[rows, cols], v_s[rows, cols], g_heads[rows, cols], live, first)
                for k in range(3):
                    g_proj[k, rows, cols] = grads[k]

    @act(keys["part"])
    def _():
        for load in loads[9:13]:
            load.wait()
        swap_two.wait_send()

        @pl.loop(0, near.shape[1] // 256)
        def _(i):
            cols = pl.ds(pl.multiple_of(i * 256, 256), 256)
            near[:, cols] = (
                dot_nt(g_proj[0, :tok_rows], wqkv[0, cols, :])
                + dot_nt(g_proj[1, :tok_rows], wqkv[1, cols, :])
                + dot_nt(g_proj[2, :tok_rows], wqkv[2, cols, :])
            )

        swap_one.start()
        zero = jnp.zeros((1, g_proj.shape[2]), F32)
        sums = each_block(
            g_proj.shape[1], 16,
            lambda at, c: tuple(s + fold(g_proj[k, at, :].astype(F32)) for s, k in zip(c, (0, 2))), (zero, zero))
        small[8:9, : g_proj.shape[2]] = sums[0]
        small[8:9, g_proj.shape[2] :] = sums[1]

    own_mlp = pltpu.make_async_copy(mlp_hbm, near, in_sem.at[0])
    put_tok = pltpu.make_async_copy(cot, o_tok, fin_sem.at[0])
    put_layer = pltpu.make_async_copy(tok, o_layer, fin_sem.at[1])

    @act(keys["one"])
    def _():
        swap_one.wait_recv()
        swap_mlp.start()
        gain = vec[9:10, :]

        def block(at, carry):
            grad = near[at, :] + far_one[at, :]
            normal, through = norm_back_rows(tok[at, :].astype(F32), grad, gain)
            cot[at, :] = (mid[at, :] + through).astype(BF16)
            return tuple(c + fold(v) for c, v in zip(carry, (grad * normal, grad)))

        zero = jnp.zeros((1, near.shape[1]), F32)
        sums = each_block(tok_rows, 16, block, (zero, zero))
        for k in range(2):
            small[k + 4 : k + 5, :] = sums[k]
        put_tok.start()
        swap_one.wait_send()
        own_mlp.start()

    @act(keys["layer"])
    def _():
        own_mlp.wait()
        swap_mlp.wait_recv()
        shift = vec[10:11, :]

        def block(at, carry):
            tok[at, :] = (after[at, :] + (near[at, :] + far[at, :]) + shift).astype(BF16)
            return carry

        each_block(tok_rows, 16, block)
        put_layer.start()

    doubles = [
        pltpu.make_async_remote_copy(
            src_ref=small, dst_ref=small_in.at[k], send_sem=v_send.at[k], recv_sem=v_recv.at[k],
            device_id=target, device_id_type=MESH,
        )
        for k, target in enumerate((to_core, to_y, to_z, to_far))
    ]
    for k in range(5):
        @act(keys["small"][k])
        def _(k=k):
            if k:
                doubles[k - 1].wait()
                small[...] = small[...] + small_in[k - 1]
            if k < 4:
                doubles[k].start()
            else:
                put_small.start()

    put_small = pltpu.make_async_copy(small, o_small, fin_sem.at[2])

    for _, _, fn in sorted(actions, key=lambda t: t[:2]):
        fn()
    swap_mlp.wait_send()
    for copy in (put_tok, put_layer, put_small):
        copy.wait()
    for end in ends:
        end()


KEYS = {
    "lag": 0.4, "ahead": 0.8,
    "p": (0, 2.0, 3.5, 5.0, 6.5, 8.0), "r": (0, 2.0, 3.3, 4.7, 6.0, 8.0),
    "two": 3.0, "attn": (3.3, 3.6, 3.9), "part": 4.2, "one": 8.0, "layer": 10.6,
    "small": (9.0, 9.5, 10.0, 10.5, 11.0),
}


def backward(args, group, keys=KEYS):
    g_fc2, g_fc1 = args[0], args[1]
    tok_rows, width = args[2].shape
    cols = args[7].shape[1]
    pad_rows = args[7].shape[0]
    shapes = [g_fc2.shape, g_fc1.shape, (width, cols), (cols, width), (width, cols), (width, cols)]
    layout = split_plan(shapes)
    slots, at = [], 0.0
    for m, c, count in layout:
        slots.append([at + j for j in range(count)])
        at += count
    scratch, units = [], 0
    for m, c, count in layout:
        units += 2 * count
        n, h = m // 2, m // 4
        for lead, rows in ((2 * count, n), (count, h), (count, h), (count, h), (count, n), (count, h), (count, h)):
            scratch.append(pltpu.VMEM((lead, rows, c), F32))
    dma = pltpu.SemaphoreType.DMA
    scratch += [
        pltpu.VMEM((tok_rows, width), F32), pltpu.VMEM((tok_rows, width), F32), pltpu.VMEM((tok_rows, width), F32),
        pltpu.VMEM((tok_rows, width), F32), pltpu.VMEM((tok_rows, width), F32), pltpu.VMEM((pad_rows, width), BF16),
        pltpu.VMEM((pad_rows, cols), BF16), pltpu.VMEM((pad_rows, cols), BF16), pltpu.VMEM((pad_rows, cols), BF16),
        pltpu.VMEM((pad_rows, cols), BF16), pltpu.VMEM((3, pad_rows, cols), BF16), pltpu.VMEM((cols, width), BF16),
        pltpu.VMEM((3, width, cols), BF16), pltpu.VMEM((width, pad_rows), BF16), pltpu.VMEM((cols, pad_rows), BF16),
        pltpu.VMEM((tok_rows, width), BF16), pltpu.VMEM((tok_rows, width), BF16), pltpu.VMEM(args[10].shape, F32),
        pltpu.VMEM((16, width), F32), pltpu.VMEM((16, width), F32), pltpu.VMEM((4, 16, width), F32),
        pltpu.VMEM((2, layout[0][0] // 2, layout[0][1]), F32), pltpu.VMEM((2, layout[1][0] // 2, layout[1][1]), F32),
        pltpu.VMEM((2, layout[2][0] // 2, layout[2][1]), F32),
        pltpu.SemaphoreType.REGULAR((units,)), dma((units, 7)), dma((units, 7)), dma((units, 2)), dma((units, 2)), dma((units, 2)),
        dma((13,)), dma((2, 2)), dma((3,)), dma((3,)), dma((4,)), dma((4,)), dma((3,)),
    ]
    spec = pl.BlockSpec(memory_space=pl.ANY)
    shape = jax.ShapeDtypeStruct
    return pl.pallas_call(
        functools.partial(back_kernel, layout, keys, slots, group),
        out_shape=[shape(s, F32) for s in shapes]
        + [shape((tok_rows, width), BF16), shape((tok_rows, width), BF16), shape((16, width), F32)],
        in_specs=[spec] * 16,
        out_specs=[spec] * 9,
        scratch_shapes=scratch,
        name="backward",
        compiler_params=pltpu.CompilerParams(
            collective_id=0, has_side_effects=True, vmem_limit_bytes=67043328
        ),
    )(*args)


def make_body(n_dp, n_mp):
    fast = n_dp == 16 and n_mp == 2

    def sum_mp(part):
        if n_mp == 2:
            return part + swap(part, "mp", 2, 1)
        return lax.psum(part, "mp")

    def body(
        tokens, keep_mask, ln1_gain, ln1_bias, w_qkv, b_qkv, w_proj, b_proj,
        ln2_gain, ln2_bias, w_fc1, b_fc1, w_fc2, b_fc2, cotangent,
    ):
        inputs = tokens.astype(F32)
        tok_rows, width = inputs.shape
        images = keep_mask.shape[0]
        slots = tok_rows // images
        cols = w_qkv.shape[2]
        heads = cols // HEAD
        shape = (images, slots, heads, HEAD)

        normal_one, inverse_one = norm_parts(inputs)
        norm_one = (normal_one * ln1_gain + ln1_bias).astype(BF16)
        weight = w_qkv.transpose(1, 0, 2)
        query = (dot_nn(norm_one, weight[0]) + b_qkv[0]).astype(BF16).reshape(shape)
        keys = dot_nn(norm_one, weight[1]).astype(BF16).reshape(shape)
        values = (dot_nn(norm_one, weight[2]) + b_qkv[1]).astype(BF16).reshape(shape)
        scores = jnp.einsum("bqhd,bkhd->bhqk", query, keys, preferred_element_type=F32) * 0.125
        live = (keep_mask > 0)[:, None, None, :]
        masked = jnp.where(live, scores, -1e30)
        row_max = jnp.max(masked, axis=-1, keepdims=True)
        exp_terms = jnp.where(live, jnp.exp(masked - row_max), 0.0)
        probs = exp_terms / jnp.sum(exp_terms, axis=-1, keepdims=True)
        probs_low = probs.astype(BF16)
        mixed = jnp.einsum("bhqk,bkhd->bqhd", probs_low, values, preferred_element_type=F32)
        heads_out = mixed.reshape(tok_rows, cols).astype(BF16)
        after_attn = inputs + sum_mp(dot_nn(heads_out, w_proj)) + b_proj

        normal_two, inverse_two = norm_parts(after_attn)
        norm_two = (normal_two * ln2_gain + ln2_bias).astype(BF16)
        pre_act = dot_nn(norm_two, w_fc1) + b_fc1
        hidden_f, gelu_back = jax.vjp(lambda v: jax.nn.gelu(v, approximate=False), pre_act)
        hidden = hidden_f.astype(BF16)
        grad_w_fc2 = dot_tn(hidden, cotangent)
        grad_pre = gelu_back(dot_nt(cotangent, w_fc2))[0].astype(BF16)
        norm_two_part = dot_nt(grad_pre, w_fc1)
        grad_w_fc1 = dot_tn(norm_two, grad_pre)
        mlp_part = dot_nn(hidden, w_fc2)
        grad_out = cotangent.astype(F32)
        sum_out = jnp.sum(grad_out, axis=0)
        sum_pre = jnp.sum(grad_pre.astype(F32), axis=0)
        if fast:
            pad = -tok_rows % 128
            group = 4 * slots
            image = jnp.arange(tok_rows + pad) // slots
            place = jnp.arange(256)
            base = jnp.arange(tok_rows + pad) // group * 4
            key_image = base[:, None] + place[None, :] // slots
            kept = jnp.pad(keep_mask, ((0, 2), (0, 0)))
            rows_kept = jnp.concatenate(
                [
                    jnp.broadcast_to(kept[4 * g : 4 * g + 4].reshape(1, group), (size, group))
                    for g, size in enumerate((group, group, tok_rows + pad - 2 * group))
                ]
            )
            rows_kept = jnp.pad(rows_kept, ((0, 0), (0, 256 - group)))
            live_map = ((image[:, None] == key_image) & (rows_kept > 0)).astype(F32)
            vec = jnp.concatenate(
                [
                    ln2_gain,
                    jnp.zeros(5 * width, F32),
                    sum_pre,
                    jnp.zeros(width, F32),
                    ln1_gain,
                    b_fc2,
                    sum_out,
                    jnp.zeros(4 * width, F32),
                ]
            ).reshape(16, width)
            padded = lambda v: jnp.pad(v.reshape(tok_rows, -1), ((0, pad), (0, 0)))
            results = backward(
                (
                    grad_w_fc2,
                    grad_w_fc1,
                    norm_two_part,
                    mlp_part,
                    after_attn,
                    tokens,
                    cotangent,
                    padded(query),
                    padded(keys),
                    padded(values),
                    live_map,
                    w_proj,
                    weight,
                    padded(norm_one).T,
                    padded(heads_out).T,
                    vec,
                ),
                group,
            )
            grad_w_fc2, grad_w_fc1, grad_w_v, grad_w_proj, grad_w_q, grad_w_k = results[:6]
            layer_out, grad_tokens, small = results[6:]
            return (
                layer_out,
                grad_tokens,
                small[4],
                small[5],
                jnp.stack([grad_w_q, grad_w_k, grad_w_v], axis=1),
                small[8].reshape(2, cols),
                grad_w_proj,
                small[3],
                small[1],
                small[2],
                grad_w_fc1,
                small[6:8].reshape(-1),
                grad_w_fc2,
                small[11],
            )

        grad_norm_two = sum_mp(norm_two_part)
        layer_out = (after_attn + sum_mp(mlp_part) + b_fc2).astype(BF16)
        grad_mid = grad_out + norm_back(grad_norm_two, normal_two, inverse_two, ln2_gain)
        grad_mid_low = grad_mid.astype(BF16)
        grad_heads = dot_nt(grad_mid_low, w_proj).astype(BF16).reshape(shape)
        grad_w_proj = dot_tn(heads_out, grad_mid_low)
        grad_probs = jnp.einsum("bqhd,bkhd->bhqk", grad_heads, values, preferred_element_type=F32)
        grad_values = jnp.einsum(
            "bhqk,bqhd->bkhd", probs_low, grad_heads, preferred_element_type=F32
        ).astype(BF16)
        inner = jnp.sum(probs * grad_probs, axis=-1, keepdims=True)
        grad_scores = (probs * (grad_probs - inner)).astype(BF16)
        grad_query = (
            jnp.einsum("bhqk,bkhd->bqhd", grad_scores, keys, preferred_element_type=F32) * 0.125
        ).astype(BF16)
        grad_keys = (
            jnp.einsum("bhqk,bqhd->bkhd", grad_scores, query, preferred_element_type=F32) * 0.125
        ).astype(BF16)
        grad_query = grad_query.reshape(tok_rows, cols)
        grad_keys = grad_keys.reshape(tok_rows, cols)
        grad_values = grad_values.reshape(tok_rows, cols)
        part = (
            dot_nt(grad_query, weight[0])
            + dot_nt(grad_keys, weight[1])
            + dot_nt(grad_values, weight[2])
        )
        grad_norm_one = sum_mp(part)
        grads = [
            grad_w_fc2,
            grad_w_fc1,
            grad_w_proj,
            dot_tn(norm_one, grad_values),
            dot_tn(norm_one, grad_query),
            dot_tn(norm_one, grad_keys),
        ]
        grads = lax.psum(grads, "dp")
        grad_w_fc2, grad_w_fc1, grad_w_proj, grad_w_v, grad_w_q, grad_w_k = grads
        grad_w_qkv = jnp.stack([grad_w_q, grad_w_k, grad_w_v], axis=1)
        grad_tokens = (
            grad_mid + norm_back(grad_norm_one, normal_one, inverse_one, ln1_gain)
        ).astype(BF16)

        small = jnp.concatenate(
            [
                sum_out,
                jnp.sum(grad_norm_two * normal_two, axis=0),
                jnp.sum(grad_norm_two, axis=0),
                jnp.sum(grad_mid, axis=0),
                jnp.sum(grad_norm_one * normal_one, axis=0),
                jnp.sum(grad_norm_one, axis=0),
                sum_pre,
                jnp.sum(grad_query.astype(F32), axis=0),
                jnp.sum(grad_values.astype(F32), axis=0),
            ]
        )
        small = lax.psum(small, "dp")
        rows = [small[k * width : (k + 1) * width] for k in range(6)]
        spot = 6 * width + b_fc1.shape[0]
        return (
            layer_out,
            grad_tokens,
            rows[4],
            rows[5],
            grad_w_qkv,
            small[spot:].reshape(2, cols),
            grad_w_proj,
            rows[3],
            rows[1],
            rows[2],
            grad_w_fc1,
            small[6 * width : spot],
            grad_w_fc2,
            rows[0],
        )

    return body


def solution(mesh):
    return jax.shard_map(
        make_body(mesh.shape["dp"], mesh.shape["mp"]),
        mesh=mesh,
        in_specs=(
            P("dp", None),
            P("dp", None),
            P(),
            P(),
            P(None, None, "mp"),
            P(None, "mp"),
            P("mp", None),
            P(),
            P(),
            P(),
            P(None, "mp"),
            P("mp"),
            P("mp", None),
            P(),
            P("dp", None),
        ),
        out_specs=(
            P("dp", None),
            P("dp", None),
            P(),
            P(),
            P(None, None, "mp"),
            P(None, "mp"),
            P("mp", None),
            P(),
            P(),
            P(),
            P(None, "mp"),
            P("mp"),
            P("mp", None),
            P(),
        ),
        check_vma=False,
    )
```

time: 769 us -> 445 us (0.58); the launches traced: 758 us -> 443 us
  waiting for transfers between devices: 454 us -> 30.7 us
  Pallas kernels: 0 us -> 302 us
  other arithmetic: 93.7 us -> 13.8 us
  starting transfers between devices: 80.7 us -> 2.99 us
  matrix products: 70.5 us -> 47.8 us
  local copies, waits for them, and re-layouts: 57 us -> 44.5 us
    ppermute x84 -> x1, waiting for transfers between devices: 454 us -> 30.7 us  [swap(): return lax.ppermute(value, axis, [(i, i ^ mask) for i in range(size)])]
    pallas_call x0 -> x1, Pallas kernels: none -> 302 us  [backward(): pl.pallas_call(functools.partial(back_kernel, layout, keys, slots, group)...]
    ppermute x84 -> x1, starting transfers between devices: 80.7 us -> 2.99 us  [swap(): return lax.ppermute(value, axis, [(i, i ^ mask) for i in range(size)])]
    select_n x35 -> x2, other arithmetic: 59 us -> 0.02 us  [the longest x1 0.01 us: body(): image = jnp.arange(tok_rows + pad) // slots]
    broadcast_in_dim x56 -> x6, local copies, waits for them, and re-layouts: 15.7 us -> 0.28 us  [body(): jnp.broadcast_to(kept[4 * g:4 * g + 4].reshape(1, group), (size, group))]
    unnamed x166 -> x63, local copies, waits for them, and re-layouts: 5.91 us -> 17.1 us
    concatenate x3 -> x1, other arithmetic: 9.57 us -> 0.04 us  [body(): jnp.concatenate([jnp.broadcast_to(kept[4 * g:4 * g + 4].reshape(1, group)...]
    reshape x5 -> x1, local copies, waits for them, and re-layouts: 9.81 us -> 0.64 us  [body(): vec = jnp.concatenate([ln2_gain, jnp.zeros(5 * width, F32), sum_pre, jnp....]
  transfers between devices with their start and end apart: 84 -> 1, of which waited for: 37 -> 1; matrix products, arithmetic and copies ran while one was open for 20% -> 3% of each run, Pallas kernels for 0% -> 0%
where the time goes in v3:
time: 445 us; the launch traced here: 443 us
  Pallas kernels  302 us (68%)
  matrix products  47.8 us (11%)
  local copies, waits for them, and re-layouts  44.5 us (10%)
  waiting for transfers between devices  30.7 us (7%)
  other arithmetic  13.8 us (3%)
    pallas_call x1, Pallas kernels, backward(): pl.pallas_call(functools.partial(back_kernel, layout, keys, slots, group)...  302 us
    ppermute x1, waiting for transfers between devices, swap(): return lax.ppermute(value, axis, [(i, i ^ mask) for i in range(size)])  30.7 us
    unnamed x63, local copies, waits for them, and re-layouts  17.1 us
    dot_general x2, matrix products, dot_nt(): lax.dot_general(left, right, (((1,), (1,)), ((), ())), preferred_element_...  16.1 us
    dot_general x6, matrix products, dot_nn(): return jnp.dot(left, right, preferred_element_type=F32)  12.9 us
    dot_general x2, matrix products, dot_tn(): lax.dot_general(left, right, (((0,), (0,)), ((), ())), preferred_element_...  11.7 us
  transfers between devices with their start and end apart: 1, of which 1 were waited for; matrix products, arithmetic and copies ran while one was open for 3% of the time, Pallas kernels for 0%

profile of v3, /device:TPU:0, one launch (start us, length us, event | category | flops | bytes accessed | tf_op | source)
XLA Modules:
  0.0 443.3 jit_solution(17041320252886914277)
XLA Ops:
  12.2 4.4 fusion.44
  16.6 2.8 fusion.15
  21.0 2.1 fusion.53
  23.2 3.0 collective-permute-start
  26.2 1.9 pad.26.refs_8_
  28.0 1.9 pad.27.refs_9_
  30.7 2.0 copy.56
  34.9 2.0 pad_bitcast_fusion.1.refs_14_
  37.0 2.3 pad_bitcast_fusion.refs_13_
  40.5 30.7 %collective-permute-done = f32[500,1024]{1,0:T(8,128)} collective-permute-done((f32[500,1024]{1,0:T(8,128)S(1)}, f32[500,1024]{1,0:T(8,128)}, u32[]{:S(2)}, u32[]{:S(2)}) %collective-permute-start) | collective-permute-done | bytes 2048032 | tf_op jit(solution)/shard_map/ppermute | solution.py:43
  71.2 2.9 copy.55
  74.1 2.6 fusion.39
  76.7 1.9 copy.57.refs_4_
  78.9 4.9 %fusion.37 = f32[500,2048]{1,0:T(8,128)S(1)} fusion(bf16[1024,2048]{1,0:T(8,128)(2,1)} %param.25, f32[500,1024]{0,1:T(8,128)S(1)} %get-tuple-element.36, f32[1024]{0:T(1024)S(1)} %copy-done.21, f32[1024]{0:T(1024)S(1)} %copy-done.17, f32[500]{0:T(512)S(1)} %add_rsqrt_fusion, f32[500]{0:T(512)S(1)} %broadcast_multiply_fusion), kind=kOutput, calls=%fused_computation.99 | convolution fusion | flops 2099712000 | bytes 10350496 | tf_op jit(solution)/shard_map/dot_general | solution.py:17
  83.9 12.4 %convert_reduce_fusion = (f32[2048]{0:T(1024)S(1)}, bf16[500,2048]{1,0:T(8,128)(2,1)S(1)}, f32[500,2048]{1,0:T(8,128)S(1)}) fusion(f32[500,2048]{1,0:T(8,128)S(1)} %fusion.37, f32[2048]{0:T(1024)S(1)} %copy-done.14, bf16[500,1024]{1,0:T(8,128)(2,1)S(1)} %copy-done.3, bf16[2048,1024]{1,0:T(8,128)(2,1)S(1)} %copy-done.20), kind=kOutput, calls=%fused_computation.4 | convolution fusion | flops 2173949952 | bytes 15474688 | tf_op jit(solution)/shard_map/dot_general | solution.py:25
  96.3 3.6 fusion.55.refs_2_
  100.0 5.8 %fusion.36.refs_1_ = f32[1024,2048]{1,0:T(8,128)} fusion(bf16[500,2048]{1,0:T(8,128)(2,1)S(1)} %get-tuple-element.33, f32[500,1024]{0,1:T(8,128)S(1)} %get-tuple-element.36, f32[1024]{0:T(1024)S(1)} %copy-done.21, f32[1024]{0:T(1024)S(1)} %copy-done.17, f32[500]{0:T(512)S(1)} %add_rsqrt_fusion, f32[500]{0:T(512)S(1)} %broadcast_multiply_fusion), kind=kOutput, calls=%fused_computation.98 | convolution fusion | flops 2099712000 | bytes 12496800 | tf_op jit(solution)/shard_map/dot_general | solution.py:21
  106.8 3.6 fusion.56.refs_3_
  110.5 5.8 %fusion.54.refs_0_ = f32[2048,1024]{1,0:T(8,128)} fusion(bf16[500,2048]{1,0:T(8,128)(2,1)S(1)} %multiply_convert_fusion, bf16[500,1024]{1,0:T(8,128)(2,1)S(1)} %copy-done.3), kind=kOutput, calls=%fused_computation.106 | convolution fusion | flops 2097152000 | bytes 11460608 | tf_op jit(solution)/shard_map/dot_general | solution.py:21
  117.0 302.5 %backward.1 = (f32[2048,1024]{1,0:T(8,128)}, f32[1024,2048]{1,0:T(8,128)}, f32[1024,512]{1,0:T(8,128)}, f32[512,1024]{1,0:T(8,128)}, f32[1024,512]{1,0:T(8,128)}...) custom-call(f32[2048,1024]{1,0:T(8,128)} %fusion.54.refs_0_, ...), custom_call_target="tpu_custom_call" | custom-call | tf_op jit(solution)/shard_map/backward/pallas_call | solution.py:600
  423.1 7.0 %pad_maximum_fusion = f32[1024,3,512]{2,0,1:T(8,128)} fusion(f32[1024,1,512]{2,0,1:T(8,128)} %bitcast.55, f32[1024,1,512]{2,0,1:T(8,128)} %bitcast.57, f32[1024,1,512]{2,0,1:T(8,128)} %bitcast.56), kind=kLoop, calls=%fused_computation.1 | loop fusion | flops 3145728 | bytes 12582912 | tf_op jit(solution)/shard_map/stack | solution.py:721
  433.9 4.3 copy.91
  438.1 1.8 slice-done.1
  439.9 3.4 copy.92
  (98 shorter events, 26.7 us)
Async XLA Ops:
  0.6 3.6 copy-start.13
  0.7 3.6 copy-start.15
  3.6 1.9 copy-start.4
  4.7 2.4 copy-start.1
  7.0 5.2 %copy-start.6 = (bf16[500,512]{1,0:T(8,128)(2,1)}, bf16[500,512]{1,0:T(8,128)(2,1)S(1)}, u32[]{:S(2)}) copy-start(bf16[500,512]{1,0:T(8,128)(2,1)S(1)} %fusion.17) | copy-start | bytes 1536004
  7.8 8.9 %copy-start.9 = (bf16[500,512]{1,0:T(8,128)(2,1)}, bf16[500,512]{1,0:T(8,128)(2,1)S(1)}, u32[]{:S(2)}) copy-start(bf16[500,512]{1,0:T(8,128)(2,1)S(1)} %fusion.16) | copy-start | bytes 1536004
  21.0 8.9 %copy-start.7 = (bf16[500,512]{1,0:T(8,128)(2,1)S(1)}, bf16[500,512]{1,0:T(8,128)(2,1)}, u32[]{:S(2)}) copy-start(bf16[500,512]{1,0:T(8,128)(2,1)} %copy-done.6) | copy-start | bytes 1536004
  23.1 11.4 %copy-start.12 = (s32[10,50]{1,0:T(8,128)S(1)}, s32[10,50]{1,0:T(8,128)}, u32[]{:S(2)}) copy-start(s32[10,50]{1,0:T(8,128)} %param.16) | copy-start | bytes 6004
  23.2 11.7 %copy-start.17 = (f32[1024]{0:T(1024)S(1)}, f32[1024]{0:T(1024)}, u32[]{:S(2)}) copy-start(f32[1024]{0:T(1024)} %param.23) | copy-start | bytes 12292
  23.2 48.0 %collective-permute-start = (f32[500,1024]{1,0:T(8,128)S(1)}, f32[500,1024]{1,0:T(8,128)}, u32[]{:S(2)}, u32[]{:S(2)}) collective-permute-start(f32[500,1024]{1,0:T(8,128)S(1)} %fusion.53), channel_id=1, source_target_pairs={{0,1},{1,0},{2,3},{3,2},{4,5},{5,4},{6,7},{7,6},{8,9},{9,8},{10,11... | collective-permute-start | bytes 6144008 | tf_op jit(solution)/shard_map/ppermute | solution.py:43
  34.8 4.5 %copy-start.2 = (bf16[500,1024]{1,0:T(8,128)(2,1)S(1)}, bf16[500,1024]{1,0:T(8,128)(2,1)}, u32[]{:S(2)}) copy-start(bf16[500,1024]{1,0:T(8,128)(2,1)} %refs_6_.1) | copy-start | bytes 3072004
  37.0 37.1 %copy-start.16 = (f32[1024]{0:T(1024)S(1)}, f32[1024]{0:T(1024)}, u32[]{:S(2)}) copy-start(f32[1024]{0:T(1024)} %param.22) | copy-start | bytes 12292
  76.7 2.2 copy-start.21
  78.9 5.0 %copy-start.3 = (bf16[500,1024]{1,0:T(8,128)(2,1)S(1)}, bf16[500,1024]{1,0:T(8,128)(2,1)}, u32[]{:S(2)}) copy-start(bf16[500,1024]{1,0:T(8,128)(2,1)} %refs_6_.1) | copy-start | bytes 3072004
  78.9 5.0 %copy-start.14 = (f32[2048]{0:T(1024)S(1)}, f32[2048]{0:T(1024)}, u32[]{:S(2)}) copy-start(f32[2048]{0:T(1024)} %param.26) | copy-start | bytes 24580
  78.9 5.0 %copy-start.20 = (bf16[2048,1024]{1,0:T(8,128)(2,1)S(1)}, bf16[2048,1024]{1,0:T(8,128)(2,1)}, u32[]{:S(2)}) copy-start(bf16[2048,1024]{1,0:T(8,128)(2,1)} %param.27) | copy-start | bytes 12582916
  83.9 12.4 %copy-start.19 = (bf16[1024,2048]{1,0:T(8,128)(2,1)S(1)}, bf16[1024,2048]{1,0:T(8,128)(2,1)}, u32[]{:S(2)}) copy-start(bf16[1024,2048]{1,0:T(8,128)(2,1)} %param.25) | copy-start | bytes 12582916
  110.5 5.8 %copy-start.18 = (f32[1024]{0:T(1024)S(1)}, f32[1024]{0:T(1024)}, u32[]{:S(2)}) copy-start(f32[1024]{0:T(1024)} %param.28) | copy-start | bytes 12292
  423.0 7.0 %copy-start.11 = (bf16[500,1024]{1,0:T(8,128)(2,1)S(1)}, bf16[500,1024]{1,0:T(8,128)(2,1)}, u32[]{:S(2)}) copy-start(bf16[500,1024]{1,0:T(8,128)(2,1)} %get-tuple-element.67) | copy-start | bytes 3072004
  423.0 7.9 %copy-start.10 = (bf16[500,1024]{1,0:T(8,128)(2,1)S(1)}, bf16[500,1024]{1,0:T(8,128)(2,1)}, u32[]{:S(2)}) copy-start(bf16[500,1024]{1,0:T(8,128)(2,1)} %get-tuple-element.68) | copy-start | bytes 3072004
  423.1 10.8 %copy-start = (f32[1024,2048]{1,0:T(8,128)S(1)}, f32[1024,2048]{1,0:T(8,128)}, u32[]{:S(2)}) copy-start(f32[1024,2048]{1,0:T(8,128)} %get-tuple-element.77) | copy-start | bytes 25165828
  430.0 2.5 copy-start.5
  432.5 5.6 %slice-start = ((s8[8388608]{0:T(1024)(128)(4,1)}), s8[4194304]{0:T(1024)(128)(4,1)S(1)}, s32[]{:S(2)}) async-start(s8[8388608]{0:T(1024)(128)(4,1)} %bitcast.49), calls=%async_computation | async-start | bytes 8388608
  433.9 6.1 %slice-start.1 = ((s8[8388608]{0:T(1024)(128)(4,1)}), s8[4194304]{0:T(1024)(128)(4,1)S(1)}, s32[]{:S(2)}) async-start(s8[8388608]{0:T(1024)(128)(4,1)} %bitcast.49), calls=%async_computation.1 | async-start | bytes 8388608
  (1 other events, 1.5 us)

commit v4 on v3

--- a/solution.py
+++ b/solution.py
@@ -101,16 +101,248 @@
     return (grad_q * 0.125).astype(BF16), (grad_k * 0.125).astype(BF16), grad_v.astype(BF16)
 
 
+def attend(q, k, v, live, first):
+    mixed = None
+    for own in (first, 1 - first):
+        own = own.astype(BF16)
+        scores = jnp.where(live, dot_nt(q * own, k) * 0.125, -1e30)
+        exp_terms = jnp.where(live, jnp.exp(scores - jnp.max(scores, axis=-1, keepdims=True)), 0.0)
+        probs = exp_terms / jnp.maximum(jnp.sum(exp_terms, axis=-1, keepdims=True), 1.0)
+        part = dot_nn(probs.astype(BF16), v * own)
+        mixed = part if mixed is None else mixed + part
+    return mixed
+
+
+def groups_of(tok_rows, pad_rows, group):
+    starts = list(range(0, tok_rows, group))
+    return [(a, b - a) for a, b in zip(starts, starts[1:] + [pad_rows])]
+
+
+def front_kernel(slots, group, *refs):
+    (tok_hbm, kept_hbm, wqkv_hbm, wproj_hbm, wfc1_hbm, wfc2_hbm, cot_hbm, vec_hbm) = refs[:8]
+    outs = refs[8:21]
+    (tok, kept, wqkv, wproj, wfc1, wfc2, cot, vec,
+     n1, q_s, k_s, v_s, heads, live_s, after, n2, hidden, g_pre, near, mlp,
+     h_all, w_all, w_wide, w_got, h_send, h_got,
+     in_sem, out_sem, w_send, w_recv, g_send, g_recv) = refs[21:]
+    me, mp = lax.axis_index("dp"), lax.axis_index("mp")
+    core, y = me % 2, (me // 2) % 2
+    to_core = (me + 1 - 2 * core, mp)
+    to_y = (me + 2 - 4 * y, mp)
+    to_x = (me, 1 - mp)
+    tok_rows, width = tok.shape
+    pad_rows, cols = q_s.shape
+    quarter = w_wide.shape[0]
+
+    loads = [
+        pltpu.make_async_copy(src, dst, in_sem.at[i])
+        for i, (src, dst) in enumerate((
+            (wproj_hbm, wproj), (tok_hbm, tok), (vec_hbm, vec), (kept_hbm, kept), (wqkv_hbm, wqkv),
+            (wfc1_hbm, wfc1), (wfc2_hbm, wfc2), (cot_hbm, cot),
+        ))
+    ]
+    for load in loads:
+        load.start()
+    barrier = pltpu.get_barrier_semaphore()
+    for target in (to_core, to_y, to_x):
+        pl.semaphore_signal(barrier, inc=1, device_id=target, device_id_type=MESH)
+
+    def remote(src, dst, send, recv, index, target):
+        return pltpu.make_async_remote_copy(
+            src_ref=src, dst_ref=dst, send_sem=send.at[index], recv_sem=recv.at[index],
+            device_id=target, device_id_type=MESH,
+        )
+
+    place = core * 2 + y
+    w_steps = (
+        remote(w_wide, w_got.at[place], w_send, w_recv, 0, to_x),
+        remote(w_got.at[place], w_got.at[place], w_send, w_recv, 1, to_y),
+        remote(w_got.at[pl.ds(core * 2, 2)], w_got.at[pl.ds(core * 2, 2)], w_send, w_recv, 2, to_core),
+    )
+    loads[0].wait()
+    w_wide[...] = wproj[rows_at(place * quarter, quarter), :].astype(F32)
+    pl.semaphore_wait(barrier, 3)
+    w_steps[0].start()
+
+    for load in loads[1:3]:
+        load.wait()
+    n1[pl.ds(tok_rows // 16 * 16, 16), :] = jnp.zeros((16, width), BF16)
+    n2[pl.ds(tok_rows // 16 * 16, 16), :] = jnp.zeros((16, width), BF16)
+
+    def norm_block(src, dst, gain, shift):
+        def block(at, carry):
+            normal, _ = norm_parts(src[at, :].astype(F32))
+            dst[at, :] = (normal * gain + shift).astype(BF16)
+            return carry
+
+        each_block(tok_rows, 16, block)
+
+    norm_block(tok, n1, vec[9:10, :], vec[3:4, :])
+    loads[4].wait()
+    for i, dst in enumerate((q_s, k_s, v_s)):
+        @pl.loop(0, cols // 256)
+        def _(t):
+            at = pl.ds(pl.multiple_of(t * 256, 256), 256)
+            value = dot_nn(n1[...], wqkv[i, :, at])
+            if i != 1:
+                value = value + vec[4:5, pl.ds(pl.multiple_of(t * 256 + i // 2 * cols, 256), 256)]
+            dst[:, at] = value.astype(BF16)
+
+    w_steps[0].wait_recv()
+    w_steps[1].start()
+    loads[3].wait()
+    lanes = lax.broadcasted_iota(jnp.int32, (1, 128), 1)
+    first = (lanes < HEAD).astype(F32)
+    live_s[...] = jnp.zeros_like(live_s)
+    sends = []
+    for g, (start, size) in enumerate(groups_of(tok_rows, pad_rows, group)):
+        rows = pl.ds(start, size)
+        row = lax.broadcasted_iota(jnp.int32, (size, size), 0)
+        col = lax.broadcasted_iota(jnp.int32, (size, size), 1)
+        image_of = lambda v: sum((v >= slots * (k + 1)).astype(jnp.int32) for k in range(group // slots - 1))
+        same = (image_of(row) == image_of(col)).astype(F32)
+        live_s[rows, pl.ds(0, size)] = same * kept[g : g + 1, pl.ds(0, size)]
+
+        @pl.loop(0, cols // 128)
+        def _(pair):
+            at = pl.ds(pl.multiple_of(pair * 128, 128), 128)
+            live = live_s[rows, pl.ds(0, size)] > 0.0
+            mixed = attend(q_s[rows, at], k_s[rows, at], v_s[rows, at], live, first).astype(BF16)
+            heads[rows, at] = mixed
+            h_send[rows, at] = mixed.astype(F32)
+
+        send = remote(h_send.at[rows], h_got.at[rows], g_send, g_recv, g, to_x)
+        send.start()
+        sends.append(send)
+        if g == 0:
+            w_steps[1].wait_recv()
+            w_steps[2].start()
+
+    puts = []
+
+    def put(src, index):
+        copy = pltpu.make_async_copy(src, outs[index], out_sem.at[index])
+        copy.start()
+        puts.append(copy)
+
+    for index, src in enumerate((n1, q_s, k_s, v_s, heads, live_s)):
+        put(src, index)
+    mine, other = pl.ds(pl.multiple_of(mp * cols, 128), cols), pl.ds(pl.multiple_of((1 - mp) * cols, 128), cols)
+    h_all[:, mine] = heads[...]
+    w_all[mine, :] = wproj[...]
+    loads[7].wait()
+    total = each_block(
+        tok_rows, 16, lambda at, c: c + fold(cot[at, :].astype(F32)), jnp.zeros((1, width), F32)
+    )
+    w_steps[2].wait_recv()
+    for k in range(4):
+        w_all[pl.ds(pl.multiple_of((1 - mp) * cols + k * quarter, 128), quarter), :] = w_got[k].astype(BF16)
+    for send, (start, size) in zip(sends, groups_of(tok_rows, pad_rows, group)):
+        rows = pl.ds(start, size)
+        send.wait_recv()
+        h_all[rows, other] = h_got[rows, :].astype(BF16)
+
+    @pl.loop(0, width // 256)
+    def _(t):
+        at = pl.ds(pl.multiple_of(t * 256, 256), 256)
+        after[:, at] = (
+            tok[:, at].astype(F32) + dot_nn(h_all[:tok_rows, :], w_all[:, at]) + vec[2:3, at]
+        )
+
+    put(after, 6)
+    norm_block(after, n2, vec[0:1, :], vec[1:2, :])
+    put(n2, 7)
+    loads[5].wait()
+    loads[6].wait()
+    hidden[pl.ds(tok_rows // 16 * 16, 16), :] = jnp.zeros((16, hidden.shape[1]), BF16)
+    g_pre[pl.ds(tok_rows // 16 * 16, 16), :] = jnp.zeros((16, hidden.shape[1]), BF16)
+    per_row = width // 256
+
+    @pl.loop(0, hidden.shape[1] // 256)
+    def _(t):
+        at = pl.ds(pl.multiple_of(t * 256, 256), 256)
+        bias_row = 6 + t // per_row
+        bias_at = pl.ds(pl.multiple_of(t % per_row * 256, 256), 256)
+        bias = vec[pl.ds(bias_row, 1), bias_at]
+        sums = jnp.zeros((1, 256), F32)
+        for start in range(0, tok_rows, 256):
+            rows = pl.ds(start, min(256, tok_rows - start))
+            pre = dot_nn(n2[rows, :], wfc1[:, at]) + bias
+            cdf = 0.5 * (1.0 + lax.erf(pre * 0.7071067811865476))
+            hidden[rows, at] = (pre * cdf).astype(BF16)
+            slope = cdf + pre * (jnp.exp(pre * pre * -0.5) * 0.3989422804014327)
+            grad = (dot_nt(cot[rows, :], wfc2[at, :]) * slope).astype(BF16)
+            g_pre[rows, at] = grad
+            sums = sums + fold(grad.astype(F32))
+        vec[pl.ds(bias_row, 1), bias_at] = sums
+
+    vec[11:12, :] = total
+    put(vec, 12)
+    put(g_pre, 9)
+    put(hidden, 8)
+
+    @pl.loop(0, width // 256)
+    def _(t):
+        at = pl.ds(pl.multiple_of(t * 256, 256), 256)
+        near[:, at] = dot_nt(g_pre[:tok_rows, :], wfc1[at, :])
+        mlp[:, at] = dot_nn(hidden[:tok_rows, :], wfc2[:, at])
+
+    put(near, 10)
+    put(mlp, 11)
+    for copy in w_steps:
+        copy.wait_send()
+    for send in sends:
+        send.wait_send()
+    for copy in puts:
+        copy.wait()
+
+
+def front(args, slots, group, hidden_cols):
+    tok_rows, width = args[0].shape
+    cols = args[3].shape[0]
+    pad_rows = tok_rows + -tok_rows % 128
+    low = [(pad_rows, width)] + [(pad_rows, cols)] * 4
+    outs = (
+        [(s, BF16) for s in low]
+        + [((pad_rows, 256), F32), ((tok_rows, width), F32), ((pad_rows, width), BF16)]
+        + [((pad_rows, hidden_cols), BF16)] * 2
+        + [((tok_rows, width), F32)] * 2
+        + [((16, width), F32)]
+    )
+    quarter = cols // 4
+    dma = pltpu.SemaphoreType.DMA
+    scratch = [pltpu.VMEM(a.shape, a.dtype) for a in args]
+    scratch += [pltpu.VMEM(s, d) for s, d in outs[:-1]]
+    scratch += [
+        pltpu.VMEM((pad_rows, 2 * cols), BF16), pltpu.VMEM((2 * cols, width), BF16),
+        pltpu.VMEM((quarter, width), F32), pltpu.VMEM((4, quarter, width), F32),
+        pltpu.VMEM((pad_rows, cols), F32), pltpu.VMEM((pad_rows, cols), F32),
+        dma((8,)), dma((13,)), dma((3,)), dma((3,)), dma((3,)), dma((3,)),
+    ]
+    spec = pl.BlockSpec(memory_space=pl.ANY)
+    return pl.pallas_call(
+        functools.partial(front_kernel, slots, group),
+        out_shape=[jax.ShapeDtypeStruct(s, d) for s, d in outs],
+        in_specs=[spec] * 8,
+        out_specs=[spec] * 13,
+        scratch_shapes=scratch,
+        name="front",
+        compiler_params=pltpu.CompilerParams(
+            collective_id=1, has_side_effects=True, vmem_limit_bytes=62 << 20
+        ),
+    )(*args)
+
+
 BUFFERS = 7
 
 
 def back_kernel(layout, keys, slots, group, *refs):
     (g_fc2, g_fc1, near_hbm, mlp_hbm, after_hbm, tok_hbm, cot_hbm, q_hbm, k_hbm, v_hbm, live_hbm, wproj_hbm,
-     wqkv_hbm, n1t_hbm, ht_hbm, vec_hbm) = refs[:16]
+     wqkv_hbm, n1_hbm, heads_hbm, vec_hbm) = refs[:16]
     o_fc2, o_fc1, o_v, o_proj, o_q, o_k, o_layer, o_tok, o_small = refs[16:25]
     rest = refs[25:]
     bufs = [rest[i * BUFFERS : (i + 1) * BUFFERS] for i in range(6)]
-    (near, far, far_one, after, mid, low, g_heads, q_s, k_s, v_s, g_proj, wproj, wqkv, n1t, ht, cot, tok, live_s,
+    (near, far, far_one, after, mid, low, g_heads, q_s, k_s, v_s, g_proj, wproj, wqkv, n1, heads, cot, tok, live_s,
      vec, small, small_in, st_fc2, st_fc1, st_qkv,
      free_sem, send_sem, recv_sem, out_sem, away_sem, land_sem, in_sem, st_sem, x_send, x_recv, v_send, v_recv, fin_sem,
      ) = rest[6 * BUFFERS :]
@@ -135,8 +367,8 @@
         pltpu.make_async_copy(src, dst, in_sem.at[i])
         for i, (src, dst) in enumerate((
             (near_hbm, near), (after_hbm, after), (cot_hbm, cot), (vec_hbm, vec),
-            (wproj_hbm, wproj), (q_hbm, q_s), (k_hbm, k_s), (v_hbm, v_s), (live_hbm, live_s), (ht_hbm, ht),
-            (n1t_hbm, n1t), (wqkv_hbm, wqkv), (tok_hbm, tok),
+            (wproj_hbm, wproj), (q_hbm, q_s), (k_hbm, k_s), (v_hbm, v_s), (live_hbm, live_s), (heads_hbm, heads),
+            (n1_hbm, n1), (wqkv_hbm, wqkv), (tok_hbm, tok),
         ))
     ]
     for load in loads[:4]:
@@ -197,8 +429,8 @@
 
     def product(a, start, size):
         if a == 3:
-            return dot_nn(ht[rows_at(start, size), :], low[...])
-        return dot_nn(n1t[rows_at(start, size), :], g_proj[{2: 2, 4: 0, 5: 1}[a]])
+            return dot_tn(heads[:, pl.ds(pl.multiple_of(start, 128), size)], low[...])
+        return dot_tn(n1[:, pl.ds(pl.multiple_of(start, 128), size)], g_proj[{2: 2, 4: 0, 5: 1}[a]])
 
     unit = 0
     for a, (m, cols, count) in enumerate(layout):
@@ -558,9 +790,9 @@
 
 KEYS = {
     "lag": 0.4, "ahead": 0.8,
-    "p": (0, 2.0, 3.5, 5.0, 6.5, 8.0), "r": (0, 2.0, 3.3, 4.7, 6.0, 8.0),
-    "two": 3.0, "attn": (3.3, 3.6, 3.9), "part": 4.2, "one": 8.0, "layer": 10.6,
-    "small": (9.0, 9.5, 10.0, 10.5, 11.0),
+    "p": (0, 1, 2, 3, 4, 5), "r": (0, 1.3, 2, 2.7, 3.4, 4.5),
+    "two": 3.5, "attn": (3.9, 4.4, 4.9), "part": 5.4, "one": 8.5, "layer": 12.5,
+    "small": (12.6, 13, 13.5, 14, 14.5),
 }
 
 
@@ -587,7 +819,7 @@
         pltpu.VMEM((tok_rows, width), F32), pltpu.VMEM((tok_rows, width), F32), pltpu.VMEM((pad_rows, width), BF16),
         pltpu.VMEM((pad_rows, cols), BF16), pltpu.VMEM((pad_rows, cols), BF16), pltpu.VMEM((pad_rows, cols), BF16),
         pltpu.VMEM((pad_rows, cols), BF16), pltpu.VMEM((3, pad_rows, cols), BF16), pltpu.VMEM((cols, width), BF16),
-        pltpu.VMEM((3, width, cols), BF16), pltpu.VMEM((width, pad_rows), BF16), pltpu.VMEM((cols, pad_rows), BF16),
+        pltpu.VMEM((3, width, cols), BF16), pltpu.VMEM((pad_rows, width), BF16), pltpu.VMEM((pad_rows, cols), BF16),
         pltpu.VMEM((tok_rows, width), BF16), pltpu.VMEM((tok_rows, width), BF16), pltpu.VMEM(args[10].shape, F32),
         pltpu.VMEM((16, width), F32), pltpu.VMEM((16, width), F32), pltpu.VMEM((4, 16, width), F32),
         pltpu.VMEM((2, layout[0][0] // 2, layout[0][1]), F32), pltpu.VMEM((2, layout[1][0] // 2, layout[1][1]), F32),
@@ -631,84 +863,27 @@
         heads = cols // HEAD
         shape = (images, slots, heads, HEAD)
 
-        normal_one, inverse_one = norm_parts(inputs)
-        norm_one = (normal_one * ln1_gain + ln1_bias).astype(BF16)
-        weight = w_qkv.transpose(1, 0, 2)
-        query = (dot_nn(norm_one, weight[0]) + b_qkv[0]).astype(BF16).reshape(shape)
-        keys = dot_nn(norm_one, weight[1]).astype(BF16).reshape(shape)
-        values = (dot_nn(norm_one, weight[2]) + b_qkv[1]).astype(BF16).reshape(shape)
-        scores = jnp.einsum("bqhd,bkhd->bhqk", query, keys, preferred_element_type=F32) * 0.125
-        live = (keep_mask > 0)[:, None, None, :]
-        masked = jnp.where(live, scores, -1e30)
-        row_max = jnp.max(masked, axis=-1, keepdims=True)
-        exp_terms = jnp.where(live, jnp.exp(masked - row_max), 0.0)
-        probs = exp_terms / jnp.sum(exp_terms, axis=-1, keepdims=True)
-        probs_low = probs.astype(BF16)
-        mixed = jnp.einsum("bhqk,bkhd->bqhd", probs_low, values, preferred_element_type=F32)
-        heads_out = mixed.reshape(tok_rows, cols).astype(BF16)
-        after_attn = inputs + sum_mp(dot_nn(heads_out, w_proj)) + b_proj
-
-        normal_two, inverse_two = norm_parts(after_attn)
-        norm_two = (normal_two * ln2_gain + ln2_bias).astype(BF16)
-        pre_act = dot_nn(norm_two, w_fc1) + b_fc1
-        hidden_f, gelu_back = jax.vjp(lambda v: jax.nn.gelu(v, approximate=False), pre_act)
-        hidden = hidden_f.astype(BF16)
-        grad_w_fc2 = dot_tn(hidden, cotangent)
-        grad_pre = gelu_back(dot_nt(cotangent, w_fc2))[0].astype(BF16)
-        norm_two_part = dot_nt(grad_pre, w_fc1)
-        grad_w_fc1 = dot_tn(norm_two, grad_pre)
-        mlp_part = dot_nn(hidden, w_fc2)
-        grad_out = cotangent.astype(F32)
-        sum_out = jnp.sum(grad_out, axis=0)
-        sum_pre = jnp.sum(grad_pre.astype(F32), axis=0)
         if fast:
-            pad = -tok_rows % 128
             group = 4 * slots
-            image = jnp.arange(tok_rows + pad) // slots
-            place = jnp.arange(256)
-            base = jnp.arange(tok_rows + pad) // group * 4
-            key_image = base[:, None] + place[None, :] // slots
-            kept = jnp.pad(keep_mask, ((0, 2), (0, 0)))
-            rows_kept = jnp.concatenate(
-                [
-                    jnp.broadcast_to(kept[4 * g : 4 * g + 4].reshape(1, group), (size, group))
-                    for g, size in enumerate((group, group, tok_rows + pad - 2 * group))
-                ]
+            total = -(-tok_rows // group) * group
+            kept = jnp.pad(
+                jnp.pad((keep_mask > 0).astype(F32).reshape(-1), (0, total - tok_rows)).reshape(-1, group),
+                ((0, 8 - total // group), (0, 256 - group)),
             )
-            rows_kept = jnp.pad(rows_kept, ((0, 0), (0, 256 - group)))
-            live_map = ((image[:, None] == key_image) & (rows_kept > 0)).astype(F32)
             vec = jnp.concatenate(
-                [
-                    ln2_gain,
-                    jnp.zeros(5 * width, F32),
-                    sum_pre,
-                    jnp.zeros(width, F32),
-                    ln1_gain,
-                    b_fc2,
-                    sum_out,
-                    jnp.zeros(4 * width, F32),
-                ]
+                [ln2_gain, ln2_bias, b_proj, ln1_bias, b_qkv.reshape(-1), ln1_gain, b_fc1, ln1_gain,
+                 ln1_gain, b_fc2]
+                + [jnp.zeros(5 * width, F32)]
             ).reshape(16, width)
-            padded = lambda v: jnp.pad(v.reshape(tok_rows, -1), ((0, pad), (0, 0)))
+            weight = w_qkv.transpose(1, 0, 2)
+            (norm_one, query, keys, values, heads_out, live_map, after_attn, norm_two, hidden, grad_pre,
+             norm_two_part, mlp_part, vec) = front(
+                (tokens, kept, weight, w_proj, w_fc1, w_fc2, cotangent, vec), slots, group, w_fc1.shape[1]
+            )
             results = backward(
-                (
-                    grad_w_fc2,
-                    grad_w_fc1,
-                    norm_two_part,
-                    mlp_part,
-                    after_attn,
-                    tokens,
-                    cotangent,
-                    padded(query),
-                    padded(keys),
-                    padded(values),
-                    live_map,
-                    w_proj,
-                    weight,
-                    padded(norm_one).T,
-                    padded(heads_out).T,
-                    vec,
-                ),
+                (dot_tn(hidden[:tok_rows], cotangent), dot_tn(norm_two, grad_pre), norm_two_part, mlp_part,
+                 after_attn, tokens, cotangent, query, keys, values, live_map, w_proj, weight, norm_one,
+                 heads_out, vec),
                 group,
             )
             grad_w_fc2, grad_w_fc1, grad_w_v, grad_w_proj, grad_w_q, grad_w_k = results[:6]
@@ -730,6 +905,36 @@
                 small[11],
             )
 
+        normal_one, inverse_one = norm_parts(inputs)
+        norm_one = (normal_one * ln1_gain + ln1_bias).astype(BF16)
+        weight = w_qkv.transpose(1, 0, 2)
+        query = (dot_nn(norm_one, weight[0]) + b_qkv[0]).astype(BF16).reshape(shape)
+        keys = dot_nn(norm_one, weight[1]).astype(BF16).reshape(shape)
+        values = (dot_nn(norm_one, weight[2]) + b_qkv[1]).astype(BF16).reshape(shape)
+        scores = jnp.einsum("bqhd,bkhd->bhqk", query, keys, preferred_element_type=F32) * 0.125
+        live = (keep_mask > 0)[:, None, None, :]
+        masked = jnp.where(live, scores, -1e30)
+        row_max = jnp.max(masked, axis=-1, keepdims=True)
+        exp_terms = jnp.where(live, jnp.exp(masked - row_max), 0.0)
+        probs = exp_terms / jnp.sum(exp_terms, axis=-1, keepdims=True)
+        probs_low = probs.astype(BF16)
+        mixed = jnp.einsum("bhqk,bkhd->bqhd", probs_low, values, preferred_element_type=F32)
+        heads_out = mixed.reshape(tok_rows, cols).astype(BF16)
+        after_attn = inputs + sum_mp(dot_nn(heads_out, w_proj)) + b_proj
+
+        normal_two, inverse_two = norm_parts(after_attn)
+        norm_two = (normal_two * ln2_gain + ln2_bias).astype(BF16)
+        pre_act = dot_nn(norm_two, w_fc1) + b_fc1
+        hidden_f, gelu_back = jax.vjp(lambda v: jax.nn.gelu(v, approximate=False), pre_act)
+        hidden = hidden_f.astype(BF16)
+        grad_w_fc2 = dot_tn(hidden, cotangent)
+        grad_pre = gelu_back(dot_nt(cotangent, w_fc2))[0].astype(BF16)
+        norm_two_part = dot_nt(grad_pre, w_fc1)
+        grad_w_fc1 = dot_tn(norm_two, grad_pre)
+        mlp_part = dot_nn(hidden, w_fc2)
+        grad_out = cotangent.astype(F32)
+        sum_out = jnp.sum(grad_out, axis=0)
+        sum_pre = jnp.sum(grad_pre.astype(F32), axis=0)
         grad_norm_two = sum_mp(norm_two_part)
         layer_out = (after_attn + sum_mp(mlp_part) + b_fc2).astype(BF16)
         grad_mid = grad_out + norm_back(grad_norm_two, normal_two, inverse_two, ln2_gain)

time: 445 us -> 375 us (0.84)
  matrix products: 47.8 us -> 13.3 us
  waiting for transfers between devices: 30.7 us -> 0 us
  Pallas kernels: 302 us -> 328 us
  local copies, waits for them, and re-layouts: 44.5 us -> 24.6 us
  other arithmetic: 13.8 us -> 8.26 us
    pallas_call x0 -> x1, Pallas kernels: none -> 67.7 us  [front(): pl.pallas_call(functools.partial(front_kernel, slots, group), out_shape=[...]
    pallas_call x1, Pallas kernels: 302 us -> 260 us  [backward(): pl.pallas_call(functools.partial(back_kernel, layout, keys, slots, group)...]
    dot_general x9 -> x0, matrix products: 31.7 us -> none  [the longest x2 16.1 us: dot_nt(): lax.dot_general(left, right, (((1,), (1,)), ((), ())), preferred_element_...]
    ppermute x1 -> x0, waiting for transfers between devices: 30.7 us -> none  [swap(): return lax.ppermute(value, axis, [(i, i ^ mask) for i in range(size)])]
    pad x3 -> x1, local copies, waits for them, and re-layouts: 4.55 us -> 0.01 us  [body(): jnp.pad((keep_mask > 0).astype(F32).reshape(-1), (0, total - tok_rows))]
    unnamed x63 -> x36, local copies, waits for them, and re-layouts: 17.1 us -> 21.6 us
  transfers between devices with their start and end apart: 1 -> 0, of which waited for: 1 -> 0; matrix products, arithmetic and copies ran while one was open for 3% -> 0% of each run, Pallas kernels for 0% -> 0%
where the time goes in v4:
time: 375 us; the launch traced here: 374 us
  Pallas kernels  328 us (87%)
  local copies, waits for them, and re-layouts  24.6 us (7%)
  matrix products  13.3 us (4%)
  other arithmetic  8.26 us (2%)
    pallas_call x1, Pallas kernels, backward(): pl.pallas_call(functools.partial(back_kernel, layout, keys, slots, group)...  260 us
    pallas_call x1, Pallas kernels, front(): pl.pallas_call(functools.partial(front_kernel, slots, group), out_shape=[...  67.7 us
    unnamed x36, local copies, waits for them, and re-layouts  21.6 us
    dot_general x2, matrix products, dot_tn(): lax.dot_general(left, right, (((0,), (0,)), ((), ())), preferred_element_...  13.3 us

profile of v4, /device:TPU:0, one launch (start us, length us, event | category | flops | bytes accessed | tf_op | source)
XLA Modules:
  0.0 374.4 jit_solution(10616373271134887626)
XLA Ops:
  0.6 0.7 broadcast_compare_fusion
  1.5 0.7 copy.29
  2.8 0.7 constant_dynamic-update-slice_fusion.9
  3.5 0.7 constant_dynamic-update-slice_fusion.8
  4.2 0.7 constant_dynamic-update-slice_fusion.7
  4.9 0.7 constant_dynamic-update-slice_fusion.6
  5.6 0.7 constant_dynamic-update-slice_fusion.4
  6.3 0.7 constant_dynamic-update-slice_fusion.3
  7.0 0.7 constant_dynamic-update-slice_fusion.2
  7.7 0.7 constant_dynamic-update-slice_fusion.1
  8.4 0.7 constant_dynamic-update-slice_fusion
  9.7 67.7 %front.1 = (bf16[512,1024]{1,0:T(8,128)(2,1)}, bf16[512,512]{1,0:T(8,128)(2,1)}, bf16[512,512]{1,0:T(8,128)(2,1)}, bf16[512,512]{1,0:T(8,128)(2,1)}, bf16[512,51...) custom-call(bf16[500,1024]{1,0:T(8,128)(2,1)} %refs_5_.3, ...), custom_call_target="tpu_custom_call" | custom-call | tf_op jit(solution)/shard_map/front/pallas_call | solution.py:323
  77.4 7.5 %fusion.refs_0_ = f32[2048,1024]{1,0:T(8,128)} fusion(bf16[500,1024]{1,0:T(8,128)(2,1)S(1)} %copy-done.1, bf16[512,2048]{1,0:T(8,128)(2,1)} %get-tuple-element.36), kind=kOutput, calls=%fused_computation.1 | convolution fusion | flops 2097152000 | bytes 11476992 | tf_op jit(solution)/shard_map/dot_general | solution.py:21
  84.9 5.8 %fusion.3.refs_1_ = f32[1024,2048]{1,0:T(8,128)} fusion(bf16[512,1024]{1,0:T(8,128)(2,1)S(1)} %copy-done.6, bf16[512,2048]{1,0:T(8,128)(2,1)S(1)} %copy-done.5), kind=kOutput, calls=%fused_computation.20 | convolution fusion | flops 2147483648 | bytes 11534336 | tf_op jit(solution)/shard_map/dot_general | solution.py:21
  90.7 259.9 %backward.1 = (f32[2048,1024]{1,0:T(8,128)}, f32[1024,2048]{1,0:T(8,128)}, f32[1024,512]{1,0:T(8,128)}, f32[512,1024]{1,0:T(8,128)}, f32[1024,512]{1,0:T(8,128)}...) custom-call(f32[2048,1024]{1,0:T(8,128)} %fusion.refs_0_, ...), custom_call_target="tpu_custom_call" | custom-call | tf_op jit(solution)/shard_map/backward/pallas_call | solution.py:832
  350.6 0.8 slice_bitcast_fusion
  351.4 1.6 fusion.2
  354.1 7.0 %pad_maximum_fusion = f32[1024,3,512]{2,0,1:T(8,128)} fusion(f32[1024,1,512]{2,0,1:T(8,128)} %bitcast.24, f32[1024,1,512]{2,0,1:T(8,128)} %bitcast.26, f32[1024,1,512]{2,0,1:T(8,128)} %bitcast.25), kind=kLoop, calls=%fused_computation | loop fusion | flops 3145728 | bytes 12582912 | tf_op jit(solution)/shard_map/stack | solution.py:896
  361.1 1.0 copy.48
  362.1 1.0 copy.49
  363.6 1.3 copy.50
  364.9 4.3 %copy.51 = f32[1024,2048]{1,0:T(8,128)} copy(f32[1024,2048]{1,0:T(8,128)S(1)} %copy-done) | data formatting | bytes 16777216
  369.2 1.8 slice-done.1
  371.0 3.4 copy.52
  (27 shorter events, 3.3 us)
Async XLA Ops:
  9.7 67.7 %copy-start.1 = (bf16[500,1024]{1,0:T(8,128)(2,1)S(1)}, bf16[500,1024]{1,0:T(8,128)(2,1)}, u32[]{:S(2)}) copy-start(bf16[500,1024]{1,0:T(8,128)(2,1)} %refs_6_.3) | copy-start | bytes 3072004
  77.4 7.6 %copy-start.5 = (bf16[512,2048]{1,0:T(8,128)(2,1)S(1)}, bf16[512,2048]{1,0:T(8,128)(2,1)}, u32[]{:S(2)}) copy-start(bf16[512,2048]{1,0:T(8,128)(2,1)} %get-tuple-element.38) | copy-start | bytes 6291460
  77.4 7.5 %copy-start.6 = (bf16[512,1024]{1,0:T(8,128)(2,1)S(1)}, bf16[512,1024]{1,0:T(8,128)(2,1)}, u32[]{:S(2)}) copy-start(bf16[512,1024]{1,0:T(8,128)(2,1)} %get-tuple-element.37) | copy-start | bytes 3145732
  354.1 7.0 %copy-start.4 = (bf16[500,1024]{1,0:T(8,128)(2,1)S(1)}, bf16[500,1024]{1,0:T(8,128)(2,1)}, u32[]{:S(2)}) copy-start(bf16[500,1024]{1,0:T(8,128)(2,1)} %get-tuple-element.79) | copy-start | bytes 3072004
  354.1 7.9 %copy-start.3 = (bf16[500,1024]{1,0:T(8,128)(2,1)S(1)}, bf16[500,1024]{1,0:T(8,128)(2,1)}, u32[]{:S(2)}) copy-start(bf16[500,1024]{1,0:T(8,128)(2,1)} %get-tuple-element.80) | copy-start | bytes 3072004
  354.1 10.8 %copy-start = (f32[1024,2048]{1,0:T(8,128)S(1)}, f32[1024,2048]{1,0:T(8,128)}, u32[]{:S(2)}) copy-start(f32[1024,2048]{1,0:T(8,128)} %get-tuple-element.89) | copy-start | bytes 25165828
  361.1 2.5 copy-start.2
  363.6 5.6 %slice-start = ((s8[8388608]{0:T(1024)(128)(4,1)}), s8[4194304]{0:T(1024)(128)(4,1)S(1)}, s32[]{:S(2)}) async-start(s8[8388608]{0:T(1024)(128)(4,1)} %bitcast.22), calls=%async_computation | async-start | bytes 8388608
  364.9 6.1 %slice-start.1 = ((s8[8388608]{0:T(1024)(128)(4,1)}), s8[4194304]{0:T(1024)(128)(4,1)S(1)}, s32[]{:S(2)}) async-start(s8[8388608]{0:T(1024)(128)(4,1)} %bitcast.22), calls=%async_computation.1 | async-start | bytes 8388608
